TPU v7x, 256 devices: a whole 4x4x8 slice. The times are simulated.
256 devices in a mesh: img: 64 (over x, z, y_lo), txt: 4 (over y_hi, core).
Axes of the slice: x: 4, y: 4 (y_hi: 2, y_lo: 2; y = y_hi * 2 + y_lo), z: 8, core: 2. Of those that a mesh axis runs over, the one named last changes fastest.
Arguments:
- image_tokens: bfloat16 [32768, 256], P(('img', 'txt')), may hold values from -6 to 6
- prompt_tokens: bfloat16 [6144, 256], P(('txt', 'img')), may hold values from -6 to 6
- category_ids: int32 [6144], P(('txt', 'img')), may hold values from 0 to 383, as said below
- prompt_valid: int32 [6144], P(('txt', 'img')), may hold values from 0 to 1, as said below
- image_gain: float32 [256], replicated, may hold values from 0.5 to 1.5
- prompt_gain: float32 [256], replicated, may hold values from 0.5 to 1.5
- query_weight: bfloat16 [256, 1024], replicated, may hold values from -1.7 to 1.7
- key_weight: bfloat16 [256, 1024], replicated, may hold values from -1.7 to 1.7
- image_value_weight: bfloat16 [256, 1024], replicated, may hold values from -0.375 to 0.375
- prompt_value_weight: bfloat16 [256, 1024], replicated, may hold values from -0.375 to 0.375
- image_out_weight: bfloat16 [1024, 256], replicated, may hold values from -0.1875 to 0.1875
- prompt_out_weight: bfloat16 [1024, 256], replicated, may hold values from -0.1875 to 0.1875
- image_layer_scale: float32 [256], replicated, may hold values from 1 to 4
- prompt_layer_scale: float32 [256], replicated, may hold values from 1 to 4
Outputs:
- joined_image: bfloat16 [32768, 256], P(('img', 'txt'))
- joined_prompt: bfloat16 [6144, 256], P(('txt', 'img'))
- category_embed: float32 [384, 256], replicated
Inputs may be any that keep to these rules, and one draw needn't show every extreme that they name: `category_ids`: along the prompt the ids never fall; each of the 384 categories holds between 4 and 28 consecutive tokens. `prompt_valid`: within each category the tokens marked 1 come first, and at least one token is marked 1.
All inputs are finite; a program needn't handle non-finite values.
Results may differ from a plain program's by a relative error of at most 0.009.
The roundings to bfloat16 on the way count: a program that leaves them out, or rounds other values in their place, can miss the bound.
Values may be sent and summed in bfloat16 or wider, within the bound.
No kernel may reach another device: no remote copies, remote signals or barrier semaphores. Data moves between devices by JAX's collectives and lax.ppermute only.
A program may use at most 128 MiB of HBM per device.

v0:
```python
import math

import jax
import jax.numpy as jnp
from jax import lax
from jax.sharding import Mesh
from jax.sharding import PartitionSpec as P

HD = 256
IMG = ("img_0", "img_1", "img_2")
IMG_TXT = ("img_0", "img_1", "img_2", "txt")
TXT_IMG = ("txt", "img_0", "img_1", "img_2")


EPSILON = 1e-05
MASKED = -1e30


def sent_to_all(shard, axis):
    copies = jnp.broadcast_to(shard, (lax.axis_size(axis), *shard.shape))
    return lax.all_to_all(copies, axis, split_axis=0, concat_axis=0, tiled=True)


def in_order(parts, dim):
    parts = jnp.moveaxis(parts, 0, dim)
    lengths = parts.shape
    return parts.reshape(*lengths[:dim], lengths[dim] * lengths[dim + 1], *lengths[dim + 2 :])


def gather_directly(shard, axis, dim):
    parts = sent_to_all(shard, axis)
    return in_order(parts, dim)


def in_one_piece(arrays, axis, dim, along):
    columns = [a.reshape(*a.shape[:along], -1) for a in arrays]
    both = jnp.concatenate(columns, axis=along)
    filled, at, done = (lax.all_gather(both, axis, axis=dim, tiled=True), 0, [])
    for a, column in zip(arrays, columns):
        piece = filled[..., at : at + column.shape[along]]
        done.append(piece.reshape(*piece.shape[:along], *a.shape[along:]))
        at += column.shape[along]
    return tuple(done)


def collected_together(shard, axis):
    leaves = jax.tree.leaves(shard)
    sequence = sorted(range(len(leaves)), key=lambda k: -leaves[k].size)
    width = (1, *leaves[sequence[0]].shape)[-1]
    lines = [
        jnp.pad(leaves[k].reshape(-1), (0, -leaves[k].size % width)).reshape(-1, width)
        for k in sequence
    ]
    both, at, found = (sent_to_all(jnp.concatenate(lines), axis), 0, {})
    for k, line in zip(sequence, lines):
        piece = both[:, at : at + len(line)].reshape(len(both), -1)
        found[k] = piece[:, : leaves[k].size].reshape(-1, *leaves[k].shape)
        at += len(line)
    numbers = iter(range(len(leaves)))
    return jax.tree.map(lambda _: found[next(numbers)], shard)


def joined_by_halves(pieces, combine):
    while len(jax.tree.leaves(pieces)[0]) > 1:
        pieces = jax.vmap(combine)(
            *(jax.tree.map(lambda part: part[side::2], pieces) for side in (0, 1))
        )
    return jax.tree.map(lambda part: part[0], pieces)


def joined_all(shard, axis, combine):
    pieces = collected_together(shard, axis)
    return joined_by_halves(pieces, combine)


def collected_together_2(shard, axis):
    leaves = jax.tree.leaves(shard)
    sequence = sorted(range(len(leaves)), key=lambda k: -leaves[k].size)
    width = (1, *leaves[sequence[0]].shape)[-1]
    lines = [
        jnp.pad(leaves[k].reshape(-1), (0, -leaves[k].size % width)).reshape(-1, width)
        for k in sequence
    ]
    both, at, found = (lax.all_gather(jnp.concatenate(lines), axis), 0, {})
    for k, line in zip(sequence, lines):
        piece = both[:, at : at + len(line)].reshape(len(both), -1)
        found[k] = piece[:, : leaves[k].size].reshape(-1, *leaves[k].shape)
        at += len(line)
    numbers = iter(range(len(leaves)))
    return jax.tree.map(lambda _: found[next(numbers)], shard)


def joined_all_2(shard, axes, combine):
    for axis in axes:
        pieces = collected_together_2(shard, axis)
        shard = jax.tree.map(lambda part: part[0], pieces)
        for k in range(1, lax.axis_size(axis)):
            shard = combine(shard, jax.tree.map(lambda part: part[k], pieces))
    return shard


def cut_along(shard, dim, size):
    lengths = shard.shape
    parts = shard.reshape(*lengths[:dim], size, lengths[dim] // size, *lengths[dim + 1 :])
    return jnp.moveaxis(parts, dim, 0)


def sent_and_summed(shard, axis, dim):
    size = lax.axis_size(axis)
    parts = lax.all_to_all(cut_along(shard, dim, size), axis, 0, 0, tiled=True)
    return jnp.sum(parts.astype(jnp.float32), axis=0)


def sent_and_summed_2(shard, axis, dim):
    parts = cut_along(shard, dim, lax.axis_size(axis))
    arrived = lax.all_to_all(parts, axis, split_axis=0, concat_axis=0, tiled=True)
    return arrived.sum(axis=0)


def together(arrays, axis):
    ravelled, at, done = (jnp.concatenate([a.reshape(-1) for a in arrays]), 0, [])
    total = lax.psum(ravelled, axis)
    for a in arrays:
        done.append(total[at : at + a.size].reshape(a.shape))
        at += a.size
    return tuple(done)


def normalize(tokens_in, gain_row):
    values = tokens_in.astype(jnp.float32)
    average = jnp.mean(values, axis=-1, keepdims=True)
    centered = values - average
    variance = jnp.mean(centered * centered, axis=-1, keepdims=True)
    return (centered * lax.rsqrt(variance + EPSILON) * gain_row).astype(jnp.bfloat16)


def combine_stats(left_stats, right_stats):
    highest = jnp.maximum(left_stats[0], right_stats[0])
    summed = left_stats[1] * jnp.exp(left_stats[0] - highest) + right_stats[1] * jnp.exp(
        right_stats[0] - highest
    )
    return (highest, summed)


def on_device(
    image_tokens,
    prompt_tokens,
    category_ids,
    prompt_valid,
    image_gain,
    prompt_gain,
    query_weight,
    key_weight,
    image_value_weight,
    prompt_value_weight,
    image_out_weight,
    prompt_out_weight,
    image_layer_scale,
    prompt_layer_scale,
):
    embed_width = query_weight.shape[1]
    head_count = embed_width // HD
    image_normed = normalize(image_tokens, image_gain)
    image_weights = jnp.concatenate([query_weight, image_value_weight], axis=1)
    image_projected = jnp.dot(
        gather_directly(image_normed, "txt", 0), image_weights, preferred_element_type=jnp.float32
    ).astype(jnp.bfloat16)
    prompt_normed = normalize(prompt_tokens, prompt_gain)
    prompt_weights = jnp.concatenate([key_weight, prompt_value_weight], axis=1)
    valid_marks = prompt_valid.astype(jnp.bfloat16)
    gathered, marks_all = in_one_piece((prompt_normed, valid_marks), IMG, 0, 1)
    prompt_projected = jnp.dot(gathered, prompt_weights, preferred_element_type=jnp.float32).astype(
        jnp.bfloat16
    )
    image_count = image_projected.shape[0]
    prompt_count = prompt_projected.shape[0]
    query_heads = image_projected[:, :embed_width].reshape(image_count, head_count, HD)
    image_value_heads = image_projected[:, embed_width:].reshape(image_count, head_count, HD)
    key_heads = prompt_projected[:, :embed_width].reshape(prompt_count, head_count, HD)
    prompt_value_heads = prompt_projected[:, embed_width:].reshape(prompt_count, head_count, HD)
    scores = jnp.einsum(
        "ihd,thd->hit", query_heads, key_heads, preferred_element_type=jnp.float32
    ) / math.sqrt(HD)
    is_valid = (marks_all > 0)[None, None, :]
    masked = jnp.where(is_valid, scores, MASKED)
    local_row_top = jnp.max(masked, axis=2)
    local_row_sum = jnp.sum(
        jnp.where(is_valid, jnp.exp(masked - local_row_top[:, :, None]), 0.0), axis=2
    )
    row_top, row_sum = joined_all((local_row_top, local_row_sum), "txt", combine_stats)
    local_col_top = jnp.max(scores, axis=1)
    local_col_sum = jnp.sum(jnp.exp(scores - local_col_top[:, None, :]), axis=1)
    col_top, col_sum = joined_all_2((local_col_top, local_col_sum), IMG, combine_stats)
    row_weights = jnp.where(is_valid, jnp.exp(masked - row_top[:, :, None]), 0.0).astype(
        jnp.bfloat16
    )
    col_weights = jnp.exp(scores - col_top[:, None, :]).astype(jnp.bfloat16)
    image_numer = jnp.einsum(
        "hit,thd->ihd", row_weights, prompt_value_heads, preferred_element_type=jnp.float32
    )
    image_part = (
        (image_numer / row_sum.T[:, :, None]).reshape(image_count, embed_width).astype(jnp.bfloat16)
    )
    block_rows = image_part
    image_delta = sent_and_summed(
        jnp.dot(block_rows, image_out_weight, preferred_element_type=jnp.float32).astype(
            jnp.bfloat16
        ),
        "txt",
        0,
    )
    joined_image = (image_tokens.astype(jnp.float32) + image_layer_scale * image_delta).astype(
        jnp.bfloat16
    )
    prompt_numer = jnp.einsum(
        "hit,ihd->thd", col_weights, image_value_heads, preferred_element_type=jnp.float32
    )
    prompt_part = (
        (prompt_numer / col_sum.T[:, :, None])
        .reshape(prompt_count, embed_width)
        .astype(jnp.bfloat16)
    )
    block_rows = prompt_part
    prompt_delta = sent_and_summed_2(
        jnp.dot(block_rows, prompt_out_weight, preferred_element_type=jnp.float32), IMG, 0
    )
    prompt_joined = prompt_tokens.astype(jnp.float32) + prompt_layer_scale * prompt_delta
    category_count = prompt_count * lax.axis_size("txt") // 16
    members = jnp.logical_and(
        category_ids[None, :] == jnp.arange(category_count, dtype=jnp.int32)[:, None],
        prompt_valid[None, :] > 0,
    ).astype(jnp.float32)
    category_sum = jnp.dot(members, prompt_joined)
    category_tally = jnp.sum(members, axis=1)
    category_sum, category_tally = together((category_sum, category_tally), IMG_TXT)
    category_embed = category_sum / category_tally[:, None]
    return (joined_image, prompt_joined.astype(jnp.bfloat16), category_embed)


def solution(mesh):
    finer = Mesh(
        mesh.devices.reshape(4, 8, 2, mesh.shape["txt"]), ("img_0", "img_1", "img_2", "txt")
    )
    return jax.shard_map(
        on_device,
        mesh=finer,
        in_specs=(
            P(IMG_TXT, None),
            P(TXT_IMG, None),
            P(TXT_IMG),
            P(TXT_IMG),
            P(),
            P(),
            P(),
            P(),
            P(),
            P(),
            P(),
            P(),
            P(),
            P(),
        ),
        out_specs=(P(IMG_TXT, None), P(TXT_IMG, None), P()),
        check_vma=False,
    )
```

profile of v0, /device:TPU:1, one launch (start us, length us, event | category | flops | bytes accessed | tf_op | source)
XLA Modules:
  0.0 599.6 jit_solution(7328133230477263510)
XLA Ops:
  7.2 0.0 copy-start
  7.2 1.0 convert_reduce_fusion.1
  8.2 1.0 fusion.23
  9.2 1.0 fusion.25
  10.2 0.7 broadcast_in_dim.27
  10.9 6.6 %all-to-all-start = ((bf16[4,128,256]{2,1,0:T(8,128)(2,1)}), bf16[4,128,256]{2,1,0:T(8,128)(2,1)S(1)}, u32[]{:S(2)}, u32[]{:S(2)}) async-start(bf16[4,128,256]{2,1,0:T(8,128)(2,1)} %broadcast_in_dim.27), calls=%async_computation | async-start | bytes 524288 | tf_op jit(solution)/shard_map/all_to_all | solution.py:21
  17.5 0.7 convert_bitcast_fusion
  18.1 0.1 copy.29
  18.2 0.8 convert_reduce_fusion.2
  19.1 0.9 fusion.31
  20.0 0.8 fusion.33
  20.8 136.4 %all_gather.21 = bf16[1536,257]{1,0:T(8,128)(2,1)S(1)} all-gather(bf16[24,257]{1,0:T(8,128)(2,1)S(1)} %pad_maximum_fusion.4), channel_id=1, replica_groups=mesh['img_0'=4,'img_1'=8,'img_2'=2,'txt'=4] {'img_0','img_1','img_2'}, dimensions={0}, use_global_device_ids=true | all-gather | bytes 801840 | tf_op jit(solution)/shard_map/all_gather | solution.py:38
  157.2 3.0 convolution_convert_fusion
  160.2 3.5 fusion.94
  163.8 4.8 copy.35
  168.6 0.3 compare_reduce_fusion
  168.8 0.0 all-to-all-done
  168.9 0.7 convolution_convert_fusion.1
  169.6 0.2 fusion.95
  169.8 1.0 copy-done.2
  170.7 2.5 multiply_reduce_fusion
  173.3 5.3 exponential_reduce_fusion
  178.6 0.0 copy-done.1
  178.6 0.6 broadcast_in_dim.50
  179.3 32.9 %all-to-all-start.1 = ((f32[4,8,512]{2,1,0:T(8,128)}), f32[4,8,512]{2,1,0:T(8,128)S(1)}, u32[]{:S(2)}, u32[]{:S(2)}) async-start(f32[4,8,512]{2,1,0:T(8,128)} %broadcast_in_dim.50), calls=%async_computation.1 | async-start | bytes 131072 | tf_op jit(solution)/shard_map/all_to_all | solution.py:21
  212.1 9.5 %all-gather = f32[32,1536]{1,0:T(8,128)S(1)} all-gather(f32[8,1536]{1,0:T(8,128)S(1)} %pad_maximum_fusion.1), channel_id=2, replica_groups=mesh['img_0'=4,'img_1'=8,'img_2'=2,'txt'=4] {'img_0'}, dimensions={0}, use_global_device_ids=true | all-gather | bytes 245760 | tf_op jit(solution)/shard_map/all_gather | solution.py:84
  221.7 0.1 fusion.60
  221.8 19.3 %all-gather.1 = f32[64,1536]{1,0:T(8,128)S(1)} all-gather(f32[8,1536]{1,0:T(8,128)S(1)} %pad_maximum_fusion.2), channel_id=3, replica_groups=mesh['img_0'=4,'img_1'=8,'img_2'=2,'txt'=4] {'img_1'}, dimensions={0}, use_global_device_ids=true | all-gather | bytes 442368 | tf_op jit(solution)/shard_map/all_gather | solution.py:84
  241.1 0.1 fusion.39
  241.3 3.8 all-gather.2
  245.1 0.5 copy.36
  245.7 9.1 %fusion.1 = bf16[1536,4,256]{0,2,1:T(8,128)(2,1)} fusion(f32[1536,4]{0,1:T(4,128)S(1)} %get-tuple-element.7, bf16[512,4,256]{0,2,1:T(8,128)(2,1)S(1)} %bitcast.311, f32[4,512,1536]{2,1,0:T(8,128)} %copy-done.1, f32[4,1536]{1,0:T(4,128)S(1)} %get-tuple-element.8), kind=kOutput, calls=%fused_computation.9 | convolution fusion | flops 1623195648 | bytes 16826368 | tf_op jit(solution)/shard_map/hit,ihd->thd/dot_general | solution.py:215
  254.7 5.9 copy.34
  260.6 6.1 %convert_element_type.72 = bf16[64,24,1024]{2,1,0:T(8,128)(2,1)} reshape(bf16[1536,4,256]{2,1,0:T(4,128)(2,1)} %copy.34) | data formatting | bytes 6291456 | tf_op jit(solution)/shard_map/convert_element_type | solution.py:221
  266.7 0.0 all-to-all-done.1
  266.8 0.0 copy-start.10
  266.8 8.7 %fusion.9 = bf16[512,4,256]{0,2,1:T(8,128)(2,1)S(1)} fusion(bf16[1536,4,256]{0,2,1:T(8,128)(2,1)} %bitcast.306, f32[4,512,1536]{2,1,0:T(8,128)} %copy-done.1, f32[4,512]{1,0:T(4,128)S(1)} %get-tuple-element.22, pred[1536]{0:T(1024)(128)(4,1)S(1)} %compare_reduce_fusion, f32[512,4]{0,1:T(4,128)S(1)} %get-tuple-element.21), kind=kOutput, calls=%fused_computation.19 | convolution fusion | flops 1627389952 | bytes 16795136 | tf_op jit(solution)/shard_map/hit,thd->ihd/dot_general | solution.py:198
  275.5 0.0 copy-start.11
  275.5 0.0 copy-start.8
  275.5 0.0 copy-start.3
  275.6 0.0 copy-start.9
  275.6 0.0 copy-start.6
  275.6 0.0 copy-start.7
  275.6 1.2 convolution_convert_fusion.2
  276.8 14.4 %all-to-all-start.2 = ((bf16[4,128,256]{2,1,0:T(8,128)(2,1)}), bf16[4,128,256]{2,1,0:T(8,128)(2,1)S(1)}, u32[]{:S(2)}, u32[]{:S(2)}) async-start(bf16[4,128,256]{2,1,0:T(8,128)(2,1)} %bitcast.8), calls=%async_computation.2 | async-start | bytes 524288 | tf_op jit(solution)/shard_map/all_to_all | solution.py:110
  291.2 4.0 fusion.19
  295.2 2.5 all-to-all-done.2
  297.7 4.7 all-to-all-start.3
  302.4 0.0 all-reduce.2.cloned.1.call-start
  302.5 0.0 copy-done.11
  302.5 0.1 convert_reduce_fusion.3
  302.6 0.7 fusion.26
  303.3 37.4 %all-to-all-done.3 = f32[64,24,256]{2,1,0:T(8,128)S(1)} async-done(((f32[64,24,256]{2,1,0:T(8,128)}), f32[64,24,256]{2,1,0:T(8,128)S(1)}, u32[]{:S(2)}, u32[]{:S(2)}) %all-to-all-start.3) | async-done | bytes 1572896 | tf_op jit(solution)/shard_map/all_to_all | solution.py:116
  340.7 0.1 reduce_sum.88
  340.9 0.3 convolution_bitcast_fusion
  341.2 0.2 copy.39
  341.4 0.8 pad_maximum_fusion
  342.2 0.0 all-reduce.2.cloned.1.call-update
  342.2 0.6 fusion.81
  342.8 247.2 %all-reduce.2.cloned.1.call-done = f32[98688]{0:T(1024)} async-done(((f32[98688]{0:T(1024)}), f32[98688]{0:T(1024)}) %all-reduce.2.cloned.1.call-update) | async-done | bytes 394768 | tf_op jit(solution)/shard_map/psum | solution.py:122
  590.1 1.0 slice.262
  591.1 0.1 reshape.118
  591.2 0.7 slice.263
  591.9 0.9 broadcast_divide_fusion
  (28 shorter events, 0.2 us)
Async XLA Ops:
  7.2 284.0 %copy-start = (bf16[1024,256]{1,0:T(8,128)(2,1)S(1)}, bf16[1024,256]{1,0:T(8,128)(2,1)}, u32[]{:S(2)}) copy-start(bf16[1024,256]{1,0:T(8,128)(2,1)} %param.25) | copy-start | bytes 1572868
  10.9 157.9 %all-to-all-start = ((bf16[4,128,256]{2,1,0:T(8,128)(2,1)}), bf16[4,128,256]{2,1,0:T(8,128)(2,1)S(1)}, u32[]{:S(2)}, u32[]{:S(2)}) async-start(bf16[4,128,256]{2,1,0:T(8,128)(2,1)} %broadcast_in_dim.27), calls=%async_computation | async-start | bytes 524288 | tf_op jit(solution)/shard_map/all_to_all | solution.py:21
  163.8 5.1 copy-start.4
  163.8 5.1 copy-start.5
  168.9 1.9 copy-start.2
  173.3 5.3 copy-start.1
  179.3 87.5 %all-to-all-start.1 = ((f32[4,8,512]{2,1,0:T(8,128)}), f32[4,8,512]{2,1,0:T(8,128)S(1)}, u32[]{:S(2)}, u32[]{:S(2)}) async-start(f32[4,8,512]{2,1,0:T(8,128)} %broadcast_in_dim.50), calls=%async_computation.1 | async-start | bytes 131072 | tf_op jit(solution)/shard_map/all_to_all | solution.py:21
  266.8 8.8 %copy-start.10 = (bf16[1024,256]{1,0:T(8,128)(2,1)S(1)}, bf16[1024,256]{1,0:T(8,128)(2,1)}, u32[]{:S(2)}) copy-start(bf16[1024,256]{1,0:T(8,128)(2,1)} %param.24) | copy-start | bytes 1572868
  275.5 26.9 %copy-start.11 = (s32[24]{0:T(128)S(1)}, s32[24]{0:T(128)}, u32[]{:S(2)}) copy-start(s32[24]{0:T(128)} %param.17) | copy-start | bytes 292
  275.5 27.0 %copy-start.8 = (s32[24]{0:T(128)S(1)}, s32[24]{0:T(128)}, u32[]{:S(2)}) copy-start(s32[24]{0:T(128)} %param.16) | copy-start | bytes 292
  275.5 27.1 %copy-start.3 = (bf16[128,256]{1,0:T(8,128)(2,1)S(1)}, bf16[128,256]{1,0:T(8,128)(2,1)}, u32[]{:S(2)}) copy-start(bf16[128,256]{1,0:T(8,128)(2,1)} %param.14) | copy-start | bytes 196612
  275.6 27.1 %copy-start.9 = (f32[256]{0:T(256)S(1)}, f32[256]{0:T(256)}, u32[]{:S(2)}) copy-start(f32[256]{0:T(256)} %param.26) | copy-start | bytes 3076
  275.6 65.3 %copy-start.6 = (bf16[24,256]{1,0:T(8,128)(2,1)S(1)}, bf16[24,256]{1,0:T(8,128)(2,1)}, u32[]{:S(2)}) copy-start(bf16[24,256]{1,0:T(8,128)(2,1)} %param.15) | copy-start | bytes 36868
  275.6 65.3 %copy-start.7 = (f32[256]{0:T(256)S(1)}, f32[256]{0:T(256)}, u32[]{:S(2)}) copy-start(f32[256]{0:T(256)} %param.27) | copy-start | bytes 3076
  276.8 20.9 %all-to-all-start.2 = ((bf16[4,128,256]{2,1,0:T(8,128)(2,1)}), bf16[4,128,256]{2,1,0:T(8,128)(2,1)S(1)}, u32[]{:S(2)}, u32[]{:S(2)}) async-start(bf16[4,128,256]{2,1,0:T(8,128)(2,1)} %bitcast.8), calls=%async_computation.2 | async-start | bytes 524288 | tf_op jit(solution)/shard_map/all_to_all | solution.py:110
  297.7 43.0 %all-to-all-start.3 = ((f32[64,24,256]{2,1,0:T(8,128)}), f32[64,24,256]{2,1,0:T(8,128)S(1)}, u32[]{:S(2)}, u32[]{:S(2)}) async-start(f32[64,24,256]{2,1,0:T(8,128)} %fusion.19), calls=%async_computation.3 | async-start | bytes 3145728 | tf_op jit(solution)/shard_map/all_to_all | solution.py:116
  302.4 287.7 %all-reduce.2.cloned.1.call-start = ((), (), s32[]{:S(2)}) async-start(), calls=%async_computation.4 | async-start | bytes 794624 | tf_op jit(solution)/shard_map/psum | solution.py:122
Sparse Core Ops, SparseCore 0:
  342.3 247.6 all-reduce.1
where the time goes:
time: 601 us; the launch traced here: 600 us
  waiting for transfers between devices  287 us (48%)
  blocking collectives  169 us (28%)
  starting transfers between devices  58.5 us (10%)
  matrix products  29.6 us (5%)
  local copies, waits for them, and re-layouts  25.5 us (4%)
  other arithmetic  15.3 us (3%)
  between operations  14.4 us (2%)
    psum x1, waiting for transfers between devices, together(): total = lax.psum(ravelled, axis)  247 us
    all_gather x1, blocking collectives, in_one_piece(): filled, at, done = (lax.all_gather(both, axis, axis=dim, tiled=True), 0, [])  136 us
    all_to_all x2, starting transfers between devices, sent_to_all(): return lax.all_to_all(copies, axis, split_axis=0, concat_axis=0, tiled=True)  39.4 us
    all_to_all x1, waiting for transfers between devices, sent_and_summed_2(): lax.all_to_all(parts, axis, split_axis=0, concat_axis=0, tiled=True)  37.4 us
    all_gather x3, blocking collectives, collected_together_2(): both, at, found = (lax.all_gather(jnp.concatenate(lines), axis), 0, {})  32.7 us
    all_to_all x1, starting transfers between devices, sent_and_summed(): parts = lax.all_to_all(cut_along(shard, dim, size), axis, 0, 0, tiled=True)  14.4 us
  transfers between devices with their start and end apart: 5, of which 3 were waited for; matrix products, arithmetic and copies ran while one was open for 7% of the time, Pallas kernels for 0%

commit v1 on v0

v1 whole, which is shorter than its diff:
```python
import functools
import math

import jax
import jax.numpy as jnp
from jax import lax
from jax.experimental import pallas as pl
from jax.experimental.pallas import tpu as pltpu
from jax.sharding import Mesh
from jax.sharding import PartitionSpec as P

HD = 256
CHUNK = 256
EPSILON = 1e-05
MASKED = -1e30
ALL = ("x", "z", "yl", "yh", "c")
PROMPT_ORDER = ("yh", "c", "x", "z", "yl")
PLANE = ("x", "z")
COLUMN = ("yl", "yh", "c")
BF = jnp.bfloat16
F32 = jnp.float32


def swap(parts, axes):
    return lax.all_to_all(parts, axes, split_axis=0, concat_axis=0, tiled=True)


def spread(shard, axes):
    copies = jnp.broadcast_to(shard, (lax.axis_size(axes), *shard.shape))
    return swap(copies, axes)


def normed(tokens, gain_row):
    values = tokens.astype(F32)
    centered = values - jnp.mean(values, axis=-1, keepdims=True)
    variance = jnp.mean(centered * centered, axis=-1, keepdims=True)
    return (centered * lax.rsqrt(variance + EPSILON) * gain_row).astype(BF)


def dot(left, right):
    return jnp.dot(left, right, preferred_element_type=F32)


def dot_nt(left, right):
    return lax.dot_general(left, right, (((1,), (1,)), ((), ())), preferred_element_type=F32)


def image_kernel(tokens, gain, query_w, value_wt, queries, values_t, held):
    @pl.when(pl.program_id(0) == 0)
    def _():
        held[...] = normed(tokens[...], gain[...])

    factor = math.log2(math.e) / math.sqrt(HD)
    queries[...] = (dot(held[...], query_w[...]) * factor).astype(BF)
    values_t[...] = dot_nt(value_wt[...], held[...]).astype(BF)


def attend(reduced, kept, values_t, bias, out_t, lse, head):
    for at in range(0, kept.shape[0], CHUNK):
        scores = dot_nt(reduced, kept[at : at + CHUNK])
        if bias is not None:
            scores = scores + bias
        top = jnp.max(scores, axis=0, keepdims=True)
        weights = jnp.exp2(scores - top)
        total = jnp.sum(weights, axis=0, keepdims=True)
        numer = dot(values_t, weights.astype(BF))
        out_t[:, at : at + CHUNK] = numer * (1.0 / total)
        stat = top + jnp.log2(total)
        rows = kept.shape[0] // 128
        for k in range(CHUNK // 128):
            lse[pl.ds(head * rows + at // 128 + k, 1), :] = stat[:, k * 128 : (k + 1) * 128]


def column_kernel(tokens, gain, key_w, queries, values_t, keys, out_t, lse, held):
    head = pl.program_id(0)

    @pl.when(head == 0)
    def _():
        held[...] = normed(tokens[...], gain[...])

    key = dot(held[...], key_w[...]).astype(BF)
    keys[...] = key
    attend(queries[...], key, values_t[...], None, out_t, lse, head)


def row_kernel(tokens, gain, value_wt, keys, queries, bias, out_t, lse, held):
    head = pl.program_id(0)

    @pl.when(head == 0)
    def _():
        held[...] = normed(tokens[...], gain[...])

    values_t = dot_nt(value_wt[...], held[...]).astype(BF)
    attend(keys[...], queries[...], values_t, bias[...], out_t, lse, head)


def projected(lse_all, lse, out_t, out_wt):
    gathered = lse_all[...]
    highest = jnp.max(gathered, axis=0)
    whole = highest + jnp.log2(jnp.sum(jnp.exp2(gathered - highest[None]), axis=0))
    share = jnp.exp2(lse[...] - whole)
    heads = out_t.shape[0] // HD
    rows = share.shape[0] // heads
    total = None
    for head in range(heads):
        line = jnp.concatenate(
            [share[head * rows + k : head * rows + k + 1] for k in range(rows)], axis=1
        )
        block = slice(head * HD, (head + 1) * HD)
        part = (out_t[block, :] * line).astype(BF)
        term = dot(out_wt[:, block], part)
        total = term if total is None else total + term
    return total.T.astype(BF)


def image_out_kernel(lse_all, lse, out_t, out_wt, sent):
    sent[...] = projected(lse_all, lse, out_t, out_wt)


def members_of(codes, first, count):
    wanted = 2 * (first + lax.broadcasted_iota(jnp.int32, (count, codes.shape[1]), 0)) + 1
    return jnp.where(codes == wanted, 1.0, 0.0).astype(BF)


def prompt_out_kernel(lse_all, lse, out_t, out_wt, codes, sent, sums):
    contribution = projected(lse_all, lse, out_t, out_wt)
    sent[...] = contribution
    groups = sums.shape[0] // 2
    rows = sums.shape[1]
    gathered = dot(members_of(codes[...], 0, groups * rows), contribution).astype(BF)
    for group in range(groups):
        for side in range(2):
            sums[2 * group + side] = gathered[
                group * rows : (group + 1) * rows, side * 128 : (side + 1) * 128
            ]


def category_kernel(place, arrived, codes, tokens, scale, out):
    rows = arrived.shape[1]
    group, side = place[0], place[1]
    members = members_of(codes[...], group * rows, rows)
    base = dot(members, tokens[...])
    wide = jnp.where(side == 0, base[:, :128], base[:, 128:])
    factor = jnp.where(side == 0, scale[:, :128], scale[:, 128:])
    out[0] = wide + factor * jnp.sum(arrived[...].astype(F32), axis=0)
    tally = jnp.sum(members.astype(F32), axis=1, keepdims=True)
    out[1] = jnp.broadcast_to(tally, out.shape[1:])


def block(shape, index):
    return pl.BlockSpec(shape, index)


def whole(array):
    rank = len(array.shape)
    return pl.BlockSpec(array.shape, lambda h: (0,) * rank)


def shaped(shape, dtype):
    return jax.ShapeDtypeStruct(shape, dtype)


def cost(flops, moved, exps=0):
    return pl.CostEstimate(flops=flops, bytes_accessed=moved, transcendentals=exps)


PARAMS = dict(dimension_semantics=("arbitrary",), vmem_limit_bytes=40 * 2**20)


def on_device(
    image_tokens,
    prompt_tokens,
    category_ids,
    prompt_valid,
    image_gain,
    prompt_gain,
    query_weight,
    key_weight,
    image_value_weight,
    prompt_value_weight,
    image_out_weight,
    prompt_out_weight,
    image_layer_scale,
    prompt_layer_scale,
):
    width = query_weight.shape[1]
    heads = width // HD
    depth = image_tokens.shape[1]
    planes = lax.axis_size(PLANE)
    columns = lax.axis_size(COLUMN)
    own_prompts = prompt_tokens.shape[0]
    own_images = image_tokens.shape[0]
    images = own_images * columns
    prompts = own_prompts * planes
    categories = prompts * columns // 16

    code = (2 * category_ids + prompt_valid).reshape(1, own_prompts)
    code = jnp.pad(code, ((0, 0), (0, 128 - own_prompts)))
    prompt_all = spread(prompt_tokens, PLANE).reshape(prompts, depth)
    image_all = spread(image_tokens, COLUMN).reshape(images, depth)
    codes = spread(code, PLANE)[:, 0, :own_prompts].reshape(1, prompts)
    bias = jnp.where(codes % 2 == 1, 0.0, MASKED).astype(F32).reshape(prompts, 1)

    image_value_wt = image_value_weight.T
    prompt_value_wt = prompt_value_weight.T
    image_out_wt = image_out_weight.T
    prompt_out_wt = prompt_out_weight.T

    head_columns = lambda n: block((n, HD), lambda h: (0, h))
    head_rows = lambda n: block((HD, n), lambda h: (h, 0))

    queries, image_values_t = pl.pallas_call(
        image_kernel,
        grid=(heads,),
        in_specs=[
            whole(image_all),
            block((1, depth), lambda h: (0, 0)),
            head_columns(depth),
            head_rows(depth),
        ],
        out_specs=[head_columns(images), head_rows(images)],
        out_shape=[shaped((images, width), BF), shaped((width, images), BF)],
        scratch_shapes=[pltpu.VMEM((images, depth), BF)],
        compiler_params=pltpu.CompilerParams(**PARAMS),
        cost_estimate=cost(4 * images * depth * width, 6 * images * width),
        name="image_projection",
    )(image_all, image_gain.reshape(1, depth), query_weight, image_value_wt)

    pair_flops = 4 * images * prompts * width
    stat_rows = heads * prompts // 128
    keys, prompt_part_t, col_lse = pl.pallas_call(
        column_kernel,
        grid=(heads,),
        in_specs=[
            whole(prompt_all),
            block((1, depth), lambda h: (0, 0)),
            head_columns(depth),
            head_columns(images),
            head_rows(images),
        ],
        out_specs=[
            head_columns(prompts),
            head_rows(prompts),
            block((stat_rows, 128), lambda h: (0, 0)),
        ],
        out_shape=[
            shaped((prompts, width), BF),
            shaped((width, prompts), F32),
            shaped((stat_rows, 128), F32),
        ],
        scratch_shapes=[pltpu.VMEM((prompts, depth), BF)],
        compiler_params=pltpu.CompilerParams(**PARAMS),
        cost_estimate=cost(pair_flops, 6 * images * width, images * prompts * heads),
        name="column_attention",
    )(prompt_all, prompt_gain.reshape(1, depth), key_weight, queries, image_values_t)

    col_lse_all = spread(col_lse, PLANE)

    row_stat_rows = heads * images // 128
    image_part_t, row_lse = pl.pallas_call(
        row_kernel,
        grid=(heads,),
        in_specs=[
            whole(prompt_all),
            block((1, depth), lambda h: (0, 0)),
            head_rows(depth),
            head_columns(prompts),
            head_columns(images),
            block((prompts, 1), lambda h: (0, 0)),
        ],
        out_specs=[
            head_rows(images),
            block((row_stat_rows, 128), lambda h: (0, 0)),
        ],
        out_shape=[
            shaped((width, images), F32),
            shaped((row_stat_rows, 128), F32),
        ],
        scratch_shapes=[pltpu.VMEM((prompts, depth), BF)],
        compiler_params=pltpu.CompilerParams(**PARAMS),
        cost_estimate=cost(pair_flops, 6 * images * width, images * prompts * heads),
        name="row_attention",
    )(prompt_all, prompt_gain.reshape(1, depth), prompt_value_wt, keys, queries, bias)

    row_lse_all = spread(row_lse, COLUMN)

    prompt_sent, category_sent = pl.pallas_call(
        prompt_out_kernel,
        out_shape=[
            shaped((prompts, depth), BF),
            shaped((planes, 2 * categories // planes, 128), BF),
        ],
        compiler_params=pltpu.CompilerParams(vmem_limit_bytes=40 * 2**20),
        cost_estimate=cost(2 * prompts * depth * (width + categories), 6 * prompts * width),
        name="prompt_projection_out",
    )(col_lse_all, col_lse, prompt_part_t, prompt_out_wt, codes)

    category_arrived = swap(category_sent, PLANE)
    prompt_arrived = swap(prompt_sent.reshape(planes, own_prompts, depth), PLANE)

    place = lax.axis_index(PLANE)
    rows = category_arrived.shape[1]
    own_category = pl.pallas_call(
        category_kernel,
        in_specs=[pl.BlockSpec(memory_space=pltpu.SMEM)]
        + [pl.BlockSpec(memory_space=pltpu.VMEM)] * 4,
        out_shape=shaped((2, rows, 128), F32),
        compiler_params=pltpu.CompilerParams(vmem_limit_bytes=40 * 2**20),
        cost_estimate=cost(2 * rows * prompts * depth, 4 * prompts * depth),
        name="category_partial",
    )(
        jnp.stack([place // 2, place % 2]).astype(jnp.int32),
        category_arrived,
        codes,
        prompt_all,
        prompt_layer_scale.reshape(1, depth),
    )
    partials = jnp.sum(spread(own_category, COLUMN), axis=0)
    means = (partials[0] / partials[1]).astype(BF)
    mean_all = spread(means, PLANE)
    category_embed = (
        mean_all.reshape(planes // 2, 2, rows, 128)
        .transpose(0, 2, 1, 3)
        .reshape(categories, depth)
        .astype(F32)
    )

    image_sent = pl.pallas_call(
        image_out_kernel,
        out_shape=shaped((images, depth), BF),
        compiler_params=pltpu.CompilerParams(vmem_limit_bytes=40 * 2**20),
        cost_estimate=cost(2 * images * depth * width, 6 * images * width),
        name="image_projection_out",
    )(row_lse_all, row_lse, image_part_t, image_out_wt)
    image_arrived = swap(image_sent.reshape(columns, own_images, depth), COLUMN)
    image_delta = jnp.sum(image_arrived.astype(F32), axis=0)
    joined_image = (image_tokens.astype(F32) + image_layer_scale * image_delta).astype(BF)

    prompt_delta = jnp.sum(prompt_arrived.astype(F32), axis=0)
    joined_prompt = (prompt_tokens.astype(F32) + prompt_layer_scale * prompt_delta).astype(BF)
    return (joined_image, joined_prompt, category_embed)


def solution(mesh):
    finer = Mesh(mesh.devices.reshape(4, 8, 2, 2, 2), ALL)
    replicated = (P(),) * 10
    return jax.shard_map(
        on_device,
        mesh=finer,
        in_specs=(P(ALL, None), P(PROMPT_ORDER, None), P(PROMPT_ORDER), P(PROMPT_ORDER), *replicated),
        out_specs=(P(ALL, None), P(PROMPT_ORDER, None), P()),
        check_vma=False,
    )
```

time: 601 us -> 188 us (0.31)
  waiting for transfers between devices: 287 us -> 34.5 us
  blocking collectives: 169 us -> 24.7 us
  matrix products: 29.6 us -> 0 us
  Pallas kernels: 0 us -> 22.8 us
  between operations: 14.4 us -> 0.96 us
  other arithmetic: 15.3 us -> 2.69 us
  local copies, waits for them, and re-layouts: 25.5 us -> 37.8 us
    psum x1 -> x0, waiting for transfers between devices: 247 us -> none  [together(): total = lax.psum(ravelled, axis)]
    all_gather x4 -> x0, blocking collectives: 169 us -> none  [the longest x1 136 us: in_one_piece(): filled, at, done = (lax.all_gather(both, axis, axis=dim, tiled=True), 0, [])]
    dot_general x8 -> x0, matrix products: 29.6 us -> none  [the longest x1 9.06 us: on_device(): jnp.einsum('hit,ihd->thd', col_weights, image_value_heads, preferred_elem...]
    unnamed x25 -> x69, local copies, waits for them, and re-layouts: 1.23 us -> 27.4 us
    all_to_all x0 -> x2, blocking collectives: none -> 24.7 us  [swap(): return lax.all_to_all(parts, axes, split_axis=0, concat_axis=0, tiled=True)]
    pallas_call x0 -> x6, Pallas kernels: none -> 22.8 us  [the longest x1 7.98 us: on_device(): pl.pallas_call(column_kernel, grid=(heads,), in_specs=[whole(prompt_all),...]
    convert_element_type x2 -> x1, local copies, waits for them, and re-layouts: 12 us -> 0.2 us  [on_device(): category_embed = mean_all.reshape(planes // 2, 2, rows, 128).transpose(0,...]
    reduce_sum x8 -> x3, other arithmetic: 9.31 us -> 0.16 us  [the longest x1 0.07 us: on_device(): image_delta = jnp.sum(image_arrived.astype(F32), axis=0)]
  transfers between devices with their start and end apart: 5 -> 8, of which waited for: 3 -> 5; matrix products, arithmetic and copies ran while one was open for 7% -> 7% of each run, Pallas kernels for 0% -> 12%
where the time goes in v1:
time: 188 us; the launch traced here: 186 us
  starting transfers between devices  62.5 us (33%)
  local copies, waits for them, and re-layouts  37.8 us (20%)
  waiting for transfers between devices  34.5 us (18%)
  blocking collectives  24.7 us (13%)
  Pallas kernels  22.8 us (12%)
  other arithmetic  2.69 us (1%)
    all_to_all x8, starting transfers between devices, swap(): return lax.all_to_all(parts, axes, split_axis=0, concat_axis=0, tiled=True)  62.5 us
    all_to_all x8, waiting for transfers between devices, swap(): return lax.all_to_all(parts, axes, split_axis=0, concat_axis=0, tiled=True)  34.5 us
    unnamed x69, local copies, waits for them, and re-layouts  27.4 us
    all_to_all x2, blocking collectives, swap(): return lax.all_to_all(parts, axes, split_axis=0, concat_axis=0, tiled=True)  24.7 us
    pallas_call x1, Pallas kernels, on_device(): pl.pallas_call(column_kernel, grid=(heads,), in_specs=[whole(prompt_all),...  7.98 us
    pallas_call x1, Pallas kernels, on_device(): pl.pallas_call(row_kernel, grid=(heads,), in_specs=[whole(prompt_all), bl...  7.22 us
    broadcast_in_dim x7, local copies, waits for them, and re-layouts, spread(): copies = jnp.broadcast_to(shard, (lax.axis_size(axes), *shard.shape))  5.28 us
  transfers between devices with their start and end apart: 8, of which 5 were waited for; matrix products, arithmetic and copies ran while one was open for 7% of the time, Pallas kernels for 12%

profile of v1, /device:TPU:1, one launch (start us, length us, event | category | flops | bytes accessed | tf_op | source)
XLA Modules:
  0.0 185.9 jit_solution(17284195530351594913)
XLA Ops:
  0.7 1.0 broadcast_in_dim.34
  1.6 0.0 copy-start.30
  1.6 0.0 copy-start.31
  1.6 0.0 copy-start.15
  1.7 15.0 %all_to_all.50 = bf16[8,128,256]{2,1,0:T(8,128)(2,1)S(1)} all-to-all(bf16[8,128,256]{2,1,0:T(8,128)(2,1)S(1)} %broadcast_in_dim.34), channel_id=1, replica_groups=mesh['x'=4,'z'=8,'yl'=2,'yh'=2,'c'=2] {'yl','yh','c'}, dimensions={0} | all-to-all | bytes 1048576 | tf_op jit(solution)/shard_map/all_to_all | solution.py:25
  16.7 1.5 broadcast_in_dim.33
  18.2 11.0 %all-to-all-start = ((bf16[32,24,256]{2,1,0:T(8,128)(2,1)}), bf16[32,24,256]{2,1,0:T(8,128)(2,1)S(1)}, u32[]{:S(2)}, u32[]{:S(2)}) async-start(bf16[32,24,256]{2,1,0:T(8,128)(2,1)} %broadcast_in_dim.33), calls=%async_computation | async-start | bytes 786432 | tf_op jit(solution)/shard_map/all_to_all | solution.py:25
  29.2 0.2 copy.45
  29.4 1.0 copy.44
  30.5 0.0 copy-start.13
  30.5 1.0 copy-done.13
  31.5 2.6 %image_projection.1 = (bf16[1024,1024]{1,0:T(8,128)(2,1)S(1)}, bf16[1024,1024]{1,0:T(8,128)(2,1)S(1)}) custom-call(bf16[1024,256]{1,0:T(8,128)(2,1)S(1)} %bitcast.35, f32[1,256]{1,0:T(1,128)S(1)} %bitcast.38, bf16[256,1024]{1,0:T(8,128)(2,1)S(1)} %copy-done.13, bf16[1024,256]{1,0:T(8,128)(2,1)S(1)} %bitcast.36), custom_call_target="tpu_custom_call" | custom-call | flops 1073741824 | bytes 6291456 | tf_op jit(solution)/shard_map/image_projection/pallas_call | solution.py:212
  34.1 1.3 copy-done.18
  35.5 1.3 copy-done.21
  36.8 3.5 %all-to-all-done = bf16[32,24,256]{2,1,0:T(8,128)(2,1)S(1)} async-done(((bf16[32,24,256]{2,1,0:T(8,128)(2,1)}), bf16[32,24,256]{2,1,0:T(8,128)(2,1)S(1)}, u32[]{:S(2)}, u32[]{:S(2)}) %all-to-all-start) | async-done | bytes 393248 | tf_op jit(solution)/shard_map/all_to_all | solution.py:25
  40.3 0.7 broadcast_in_dim.35
  41.0 8.0 %all-to-all-start.2 = ((s32[32,1,128]{2,1,0:T(1,128)}), s32[32,1,128]{2,1,0:T(1,128)}, u32[]{:S(2)}, u32[]{:S(2)}) async-start(s32[32,1,128]{2,1,0:T(1,128)} %broadcast_in_dim.35), calls=%async_computation.2 | async-start | bytes 32768 | tf_op jit(solution)/shard_map/all_to_all | solution.py:25
  49.1 1.0 copy-done.14
  50.1 1.6 copy-done.19
  51.7 1.6 copy-done.22
  53.3 8.0 %column_attention.1 = (bf16[768,1024]{1,0:T(8,128)(2,1)S(1)}, f32[1024,768]{1,0:T(8,128)S(1)}, f32[24,128]{1,0:T(8,128)S(1)}) custom-call(bf16[768,256]{1,0:T(8,128)(2,1)S(1)} %bitcast.31, f32[1,256]{1,0:T(1,128)S(1)} %bitcast.39, bf16[256,1024]{1,0:T(8,128)(2,1)S(1)} %copy-done.14, bf16[1024,1024]{1,0:T(8,128)(2,1)S(1)} %copy-done.19, ...), custom_call_target="tpu_custom_call" | custom-call | flops 3221225472 | bytes 6291456 | tf_op jit(solution)/shard_map/column_attention/pallas_call | solution.py:231
  61.3 1.1 copy-done.23
  62.4 0.8 broadcast_in_dim.39
  63.2 9.2 %all-to-all-start.5 = ((f32[32,24,128]{2,1,0:T(8,128)}), f32[32,24,128]{2,1,0:T(8,128)S(1)}, u32[]{:S(2)}, u32[]{:S(2)}) async-start(f32[32,24,128]{2,1,0:T(8,128)} %broadcast_in_dim.39), calls=%async_computation.5 | async-start | bytes 786432 | tf_op jit(solution)/shard_map/all_to_all | solution.py:25
  72.4 1.9 %fusion.5 = (s32[32,1,24]{2,1,0:T(1,128)}, s32[32,24]{1,0:T(8,128)}) fusion(s32[32,1,128]{2,1,0:T(1,128)} %all-to-all-done.2), kind=kLoop, calls=%fused_computation.19 | loop fusion | bytes 9216 | tf_op jit(solution)/shard_map/slice | solution.py:201
  74.3 1.6 reshape_squeeze.7
  76.0 1.2 fusion.2.bias
  77.1 1.0 copy-done.4
  78.1 1.0 copy-done.6
  79.2 0.7 copy-done.17
  79.9 1.6 copy-done.20
  81.4 1.4 copy-done.24
  82.9 7.2 %row_attention.1 = (f32[1024,1024]{1,0:T(8,128)S(1)}, f32[32,128]{1,0:T(8,128)S(1)}) custom-call(bf16[768,256]{1,0:T(8,128)(2,1)S(1)} %bitcast.32, f32[1,256]{1,0:T(1,128)S(1)} %bitcast.40, bf16[1024,256]{1,0:T(8,128)(2,1)S(1)} %bitcast.34, bf16[768,1024]{1,0:T(8,128)(2,1)S(1)} %copy-done.24, bf16[1024,1024]{1,0:T(8,128)(2,1)S(1)} %copy-done.20, ...), custom_call_target="tpu_custom_call" | custom-call | flops 3221225472 | bytes 6291456 | tf_op jit(solution)/shard_map/row_attention/pallas_call | solution.py:260
  90.1 2.0 %copy-done = f32[1024,1024]{1,0:T(8,128)} copy-done((f32[1024,1024]{1,0:T(8,128)}, f32[1024,1024]{1,0:T(8,128)S(1)}, u32[]{:S(2)}) %copy-start) | copy-done | bytes 4194328
  92.1 0.7 broadcast_in_dim.38
  92.7 6.0 %all-to-all-start.3 = ((f32[8,32,128]{2,1,0:T(8,128)}), f32[8,32,128]{2,1,0:T(8,128)}, u32[]{:S(2)}, u32[]{:S(2)}) async-start(f32[8,32,128]{2,1,0:T(8,128)} %broadcast_in_dim.38), calls=%async_computation.3 | async-start | bytes 262144 | tf_op jit(solution)/shard_map/all_to_all | solution.py:25
  98.7 2.0 %copy.50 = bf16[1024,256]{0,1:T(8,128)(2,1)} copy(bf16[1024,256]{1,0:T(8,128)(2,1)} %param.25) | data formatting | bytes 1048576 | tf_op args[11]
  100.8 1.4 reshape_squeeze.6.codes
  102.2 1.0 copy-done.2
  103.2 0.7 copy-done.9
  103.9 0.7 copy-done.10
  104.6 1.7 prompt_projection_out.1
  106.3 0.7 copy-done.7
  106.9 9.5 %all-to-all-start.7 = ((bf16[32,24,128]{2,1,0:T(8,128)(2,1)}), bf16[32,24,128]{2,1,0:T(8,128)(2,1)S(1)}, u32[]{:S(2)}, u32[]{:S(2)}) async-start(bf16[32,24,128]{2,1,0:T(8,128)(2,1)} %copy-done.7), calls=%async_computation.7 | async-start | bytes 393216 | tf_op jit(solution)/shard_map/all_to_all | solution.py:25
  116.5 1.2 copy.49
  117.7 2.2 %copy-done.1 = f32[1024,1024]{1,0:T(8,128)S(1)} copy-done((f32[1024,1024]{1,0:T(8,128)S(1)}, f32[1024,1024]{1,0:T(8,128)}, u32[]{:S(2)}) %copy-start.1) | copy-done | bytes 4194328
  119.9 2.6 %image_projection_out.1 = bf16[1024,256]{1,0:T(8,128)(2,1)} custom-call(f32[8,32,128]{2,1,0:T(8,128)} %all-to-all-done.3.lse_all, f32[32,128]{1,0:T(8,128)S(1)} %get-tuple-element.15.lse, f32[1024,1024]{1,0:T(8,128)S(1)} %copy-done.1, bf16[256,1024]{1,0:T(8,128)(2,1)S(1)} %bitcast.30), custom_call_target="tpu_custom_call" | custom-call | flops 536870912 | bytes 6291456 | tf_op jit(solution)/shard_map/image_projection_out/pallas_call | solution.py:328
  122.5 3.4 %all-to-all-done.7.arrived = bf16[32,24,128]{2,1,0:T(8,128)(2,1)S(1)} async-done(((bf16[32,24,128]{2,1,0:T(8,128)(2,1)}), bf16[32,24,128]{2,1,0:T(8,128)(2,1)S(1)}, u32[]{:S(2)}, u32[]{:S(2)}) %all-to-all-start.7) | async-done | bytes 196640 | tf_op jit(solution)/shard_map/all_to_all | solution.py:25
  125.9 7.4 %all-to-all-start.4 = ((bf16[8,128,256]{2,1,0:T(8,128)(2,1)}), bf16[8,128,256]{2,1,0:T(8,128)(2,1)S(1)}, u32[]{:S(2)}, u32[]{:S(2)}) async-start(bf16[8,128,256]{2,1,0:T(8,128)(2,1)} %bitcast.9), calls=%async_computation.4 | async-start | bytes 1048576 | tf_op jit(solution)/shard_map/all_to_all | solution.py:25
  133.3 0.1 pad_add_fusion.place
  133.4 0.7 category_partial.1
  134.2 8.0 %all-to-all-done.4 = bf16[8,128,256]{2,1,0:T(8,128)(2,1)S(1)} async-done(((bf16[8,128,256]{2,1,0:T(8,128)(2,1)}), bf16[8,128,256]{2,1,0:T(8,128)(2,1)S(1)}, u32[]{:S(2)}, u32[]{:S(2)}) %all-to-all-start.4) | async-done | bytes 524320 | tf_op jit(solution)/shard_map/all_to_all | solution.py:25
  142.1 9.6 %all_to_all.51 = f32[8,2,24,128]{3,2,1,0:T(8,128)S(1)} all-to-all(f32[8,2,24,128]{3,2,1,0:T(8,128)S(1)} %broadcast_in_dim.41), channel_id=1, replica_groups=mesh['x'=4,'z'=8,'yl'=2,'yh'=2,'c'=2] {'yl','yh','c'}, dimensions={0} | all-to-all | bytes 393216 | tf_op jit(solution)/shard_map/all_to_all | solution.py:25
  151.8 3.9 %all-to-all-start.6 = ((bf16[32,24,256]{2,1,0:T(8,128)(2,1)}), bf16[32,24,256]{2,1,0:T(8,128)(2,1)S(1)}, u32[]{:S(2)}, u32[]{:S(2)}) async-start(bf16[32,24,256]{2,1,0:T(8,128)(2,1)} %bitcast.11), calls=%async_computation.6 | async-start | bytes 786432 | tf_op jit(solution)/shard_map/all_to_all | solution.py:25
  155.7 0.1 convert_reduce_fusion
  155.8 11.6 %all-to-all-done.6 = bf16[32,24,256]{2,1,0:T(8,128)(2,1)S(1)} async-done(((bf16[32,24,256]{2,1,0:T(8,128)(2,1)}), bf16[32,24,256]{2,1,0:T(8,128)(2,1)S(1)}, u32[]{:S(2)}, u32[]{:S(2)}) %all-to-all-start.6) | async-done | bytes 393248 | tf_op jit(solution)/shard_map/all_to_all | solution.py:25
  167.4 0.7 broadcast_in_dim.42
  168.1 7.4 %all-to-all-start.9 = ((bf16[32,24,128]{2,1,0:T(8,128)(2,1)}), bf16[32,24,128]{2,1,0:T(8,128)(2,1)S(1)}, u32[]{:S(2)}, u32[]{:S(2)}) async-start(bf16[32,24,128]{2,1,0:T(8,128)(2,1)} %broadcast_in_dim.42), calls=%async_computation.9 | async-start | bytes 393216 | tf_op jit(solution)/shard_map/all_to_all | solution.py:25
  175.5 0.6 add_convert_fusion
  176.2 0.1 convert_reduce_fusion.1
  176.2 0.6 add_convert_fusion.1
  176.8 8.0 %all-to-all-done.9 = bf16[32,24,128]{2,1,0:T(8,128)(2,1)S(1)} async-done(((bf16[32,24,128]{2,1,0:T(8,128)(2,1)}), bf16[32,24,128]{2,1,0:T(8,128)(2,1)S(1)}, u32[]{:S(2)}, u32[]{:S(2)}) %all-to-all-start.9) | async-done | bytes 196640 | tf_op jit(solution)/shard_map/all_to_all | solution.py:25
  184.9 0.2 copy.51
  185.1 0.8 copy.54
  (51 shorter events, 0.2 us)
Async XLA Ops:
  0.6 28.6 %copy-start.25 = (bf16[256,1024]{1,0:T(8,128)(2,1)S(1)}, bf16[256,1024]{1,0:T(8,128)(2,1)}, u32[]{:S(2)}) copy-start(bf16[256,1024]{1,0:T(8,128)(2,1)} %param.22) | copy-start | bytes 1572868
  0.6 28.8 %copy-start.26 = (bf16[256,1024]{1,0:T(8,128)(2,1)S(1)}, bf16[256,1024]{1,0:T(8,128)(2,1)}, u32[]{:S(2)}) copy-start(bf16[256,1024]{1,0:T(8,128)(2,1)} %param.23) | copy-start | bytes 1572868
  1.6 28.8 %copy-start.30 = (s32[24]{0:T(128)S(1)}, s32[24]{0:T(128)}, u32[]{:S(2)}) copy-start(s32[24]{0:T(128)} %param.17) | copy-start | bytes 292
  1.6 28.8 %copy-start.31 = (s32[24]{0:T(128)S(1)}, s32[24]{0:T(128)}, u32[]{:S(2)}) copy-start(s32[24]{0:T(128)} %param.16) | copy-start | bytes 292
  1.6 28.8 %copy-start.15 = (f32[256]{0:T(256)S(1)}, f32[256]{0:T(256)}, u32[]{:S(2)}) copy-start(f32[256]{0:T(256)} %param.18) | copy-start | bytes 3076
  18.2 22.2 %all-to-all-start = ((bf16[32,24,256]{2,1,0:T(8,128)(2,1)}), bf16[32,24,256]{2,1,0:T(8,128)(2,1)S(1)}, u32[]{:S(2)}, u32[]{:S(2)}) async-start(bf16[32,24,256]{2,1,0:T(8,128)(2,1)} %broadcast_in_dim.33), calls=%async_computation | async-start | bytes 786432 | tf_op jit(solution)/shard_map/all_to_all | solution.py:25
  30.4 18.6 %copy-start.16 = (f32[256]{0:T(256)S(1)}, f32[256]{0:T(256)}, u32[]{:S(2)}) copy-start(f32[256]{0:T(256)} %param.19) | copy-start | bytes 3076
  30.5 1.0 copy-start.13
  34.1 1.4 copy-start.18
  35.5 1.3 copy-start.21
  40.3 20.9 %copy-start.3 = (bf16[32,24,256]{2,1,0:T(8,128)(2,1)}, bf16[32,24,256]{2,1,0:T(8,128)(2,1)S(1)}, u32[]{:S(2)}) copy-start(bf16[32,24,256]{2,1,0:T(8,128)(2,1)S(1)} %all-to-all-done) | copy-start | bytes 1179652
  41.0 21.4 %all-to-all-start.2 = ((s32[32,1,128]{2,1,0:T(1,128)}), s32[32,1,128]{2,1,0:T(1,128)}, u32[]{:S(2)}, u32[]{:S(2)}) async-start(s32[32,1,128]{2,1,0:T(1,128)} %broadcast_in_dim.35), calls=%async_computation.2 | async-start | bytes 32768 | tf_op jit(solution)/shard_map/all_to_all | solution.py:25
  49.0 1.0 copy-start.14
  50.1 1.6 copy-start.19
  51.7 1.6 copy-start.22
  61.3 1.2 copy-start.23
  62.4 14.7 %copy-start.8 = (f32[24,128]{1,0:T(8,128)}, f32[24,128]{1,0:T(8,128)S(1)}, u32[]{:S(2)}) copy-start(f32[24,128]{1,0:T(8,128)S(1)} %get-tuple-element.17.lse) | copy-start | bytes 36868
  63.2 28.8 %all-to-all-start.5 = ((f32[32,24,128]{2,1,0:T(8,128)}), f32[32,24,128]{2,1,0:T(8,128)S(1)}, u32[]{:S(2)}, u32[]{:S(2)}) async-start(f32[32,24,128]{2,1,0:T(8,128)} %broadcast_in_dim.39), calls=%async_computation.5 | async-start | bytes 786432 | tf_op jit(solution)/shard_map/all_to_all | solution.py:25
  77.1 1.0 copy-start.4
  78.1 1.0 copy-start.6
  79.2 0.7 copy-start.17
  79.9 1.6 copy-start.20
  81.4 1.4 copy-start.24
  90.1 2.0 %copy-start = (f32[1024,1024]{1,0:T(8,128)}, f32[1024,1024]{1,0:T(8,128)S(1)}, u32[]{:S(2)}) copy-start(f32[1024,1024]{1,0:T(8,128)S(1)} %get-tuple-element.16.out_t) | copy-start | bytes 12582916
  92.7 14.2 %all-to-all-start.3 = ((f32[8,32,128]{2,1,0:T(8,128)}), f32[8,32,128]{2,1,0:T(8,128)}, u32[]{:S(2)}, u32[]{:S(2)}) async-start(f32[8,32,128]{2,1,0:T(8,128)} %broadcast_in_dim.38), calls=%async_computation.3 | async-start | bytes 262144 | tf_op jit(solution)/shard_map/all_to_all | solution.py:25
  102.2 1.0 copy-start.2
  103.2 0.7 copy-start.9
  103.9 0.7 copy-start.10
  106.3 0.7 copy-start.7
  106.9 18.9 %all-to-all-start.7 = ((bf16[32,24,128]{2,1,0:T(8,128)(2,1)}), bf16[32,24,128]{2,1,0:T(8,128)(2,1)S(1)}, u32[]{:S(2)}, u32[]{:S(2)}) async-start(bf16[32,24,128]{2,1,0:T(8,128)(2,1)} %copy-done.7), calls=%async_computation.7 | async-start | bytes 393216 | tf_op jit(solution)/shard_map/all_to_all | solution.py:25
  117.7 2.2 %copy-start.1 = (f32[1024,1024]{1,0:T(8,128)S(1)}, f32[1024,1024]{1,0:T(8,128)}, u32[]{:S(2)}) copy-start(f32[1024,1024]{1,0:T(8,128)} %copy-done) | copy-start | bytes 12582916
  119.9 13.5 %copy-start.5 = (bf16[32,24,256]{2,1,0:T(8,128)(2,1)S(1)}, bf16[32,24,256]{2,1,0:T(8,128)(2,1)}, u32[]{:S(2)}) copy-start(bf16[32,24,256]{2,1,0:T(8,128)(2,1)} %copy-done.3) | copy-start | bytes 1179652
  119.9 13.5 %copy-start.11 = (s32[1,768]{1,0:T(1,128)S(1)}, s32[1,768]{1,0:T(1,128)}, u32[]{:S(2)}) copy-start(s32[1,768]{1,0:T(1,128)} %reshape_squeeze.6.codes) | copy-start | bytes 9220
  119.9 13.5 %copy-start.12 = (f32[256]{0:T(256)S(1)}, f32[256]{0:T(256)}, u32[]{:S(2)}) copy-start(f32[256]{0:T(256)} %param.27) | copy-start | bytes 3076
  125.9 49.6 %copy-start.27 = (bf16[128,256]{1,0:T(8,128)(2,1)S(1)}, bf16[128,256]{1,0:T(8,128)(2,1)}, u32[]{:S(2)}) copy-start(bf16[128,256]{1,0:T(8,128)(2,1)} %param.14) | copy-start | bytes 196612
  125.9 49.6 %copy-start.29 = (f32[256]{0:T(256)S(1)}, f32[256]{0:T(256)}, u32[]{:S(2)}) copy-start(f32[256]{0:T(256)} %param.26) | copy-start | bytes 3076
  125.9 16.2 %all-to-all-start.4 = ((bf16[8,128,256]{2,1,0:T(8,128)(2,1)}), bf16[8,128,256]{2,1,0:T(8,128)(2,1)S(1)}, u32[]{:S(2)}, u32[]{:S(2)}) async-start(bf16[8,128,256]{2,1,0:T(8,128)(2,1)} %bitcast.9), calls=%async_computation.4 | async-start | bytes 1048576 | tf_op jit(solution)/shard_map/all_to_all | solution.py:25
  133.4 42.8 %copy-start.28 = (bf16[24,256]{1,0:T(8,128)(2,1)S(1)}, bf16[24,256]{1,0:T(8,128)(2,1)}, u32[]{:S(2)}) copy-start(bf16[24,256]{1,0:T(8,128)(2,1)} %param.15) | copy-start | bytes 36868
  151.8 15.6 %all-to-all-start.6 = ((bf16[32,24,256]{2,1,0:T(8,128)(2,1)}), bf16[32,24,256]{2,1,0:T(8,128)(2,1)S(1)}, u32[]{:S(2)}, u32[]{:S(2)}) async-start(bf16[32,24,256]{2,1,0:T(8,128)(2,1)} %bitcast.11), calls=%async_computation.6 | async-start | bytes 786432 | tf_op jit(solution)/shard_map/all_to_all | solution.py:25
  168.1 16.8 %all-to-all-start.9 = ((bf16[32,24,128]{2,1,0:T(8,128)(2,1)}), bf16[32,24,128]{2,1,0:T(8,128)(2,1)S(1)}, u32[]{:S(2)}, u32[]{:S(2)}) async-start(bf16[32,24,128]{2,1,0:T(8,128)(2,1)} %broadcast_in_dim.42), calls=%async_computation.9 | async-start | bytes 393216 | tf_op jit(solution)/shard_map/all_to_all | solution.py:25

commit v2 on v1

v2 whole, which is shorter than its diff:
```python
import math

import jax
import jax.numpy as jnp
from jax import lax
from jax.experimental import pallas as pl
from jax.experimental.pallas import tpu as pltpu
from jax.sharding import Mesh
from jax.sharding import PartitionSpec as P


HD = 256
CHUNK = 256
EPSILON = 1e-05
MASKED = -1e30
ALL = ("x", "z", "yl", "yh", "c")
PROMPT_ORDER = ("yh", "c", "x", "z", "yl")
PLANE = ("x", "z")
COLUMN = ("yl", "yh", "c")
BF = jnp.bfloat16
F32 = jnp.float32


def swap(parts, axes):
    return lax.all_to_all(parts, axes, split_axis=0, concat_axis=0, tiled=True)


def normed(tokens, gain_row):
    values = tokens.astype(F32)
    centered = values - jnp.mean(values, axis=-1, keepdims=True)
    variance = jnp.mean(centered * centered, axis=-1, keepdims=True)
    return (centered * lax.rsqrt(variance + EPSILON) * gain_row).astype(BF)


def dot(left, right):
    return jnp.dot(left, right, preferred_element_type=F32)


def dot_nt(left, right):
    return lax.dot_general(left, right, (((1,), (1,)), ((), ())), preferred_element_type=F32)


def pack_kernel(tokens, ids, valid, out):
    peers, count, depth = out.shape[0], *tokens.shape
    groups = count // 8
    lane = lax.broadcasted_iota(jnp.int32, (8, 128), 1)
    token = lax.broadcasted_iota(jnp.int32, (8, count), 0)
    wanted = lax.broadcasted_iota(jnp.int32, (8, count), 1)
    code = jnp.zeros((8, 128), F32)
    for group in range(groups):
        chosen = wanted == token + 8 * group
        pick = lambda line: jnp.sum(
            jnp.where(chosen, line[...].astype(F32), 0.0), axis=1, keepdims=True
        )
        number, real = pick(ids), pick(valid)
        sixteens = jnp.floor(number * (1.0 / 16.0))
        code = jnp.where(lane == 8 * group, real, code)
        code = jnp.where(lane == 8 * group + 1, sixteens, code)
        code = jnp.where(lane == 8 * group + 2, number - 16.0 * sixteens, code)
    copied = lambda piece: jnp.broadcast_to(piece[None], (peers, *piece.shape))
    out[:, :count] = copied(tokens[:, :128])
    out[:, count : 2 * count] = copied(tokens[:, 128:])
    out[:, 2 * count :] = copied(code.astype(BF))


def tokens_of(packed):
    peers, rows, _ = packed.shape
    count = (rows - 8) // 2
    left = packed[:, :count].reshape(peers * count, 128)
    right = packed[:, count : 2 * count].reshape(peers * count, 128)
    return jnp.concatenate([left, right], axis=1)


def codes_of(packed):
    peers, rows, _ = packed.shape
    count = (rows - 8) // 2
    code = packed[:, 2 * count :].astype(F32)
    groups = [code] + [pltpu.roll(code, 128 - 8 * k, 2) for k in range(1, count // 8)]
    return jnp.concatenate(groups, axis=1).reshape(peers * count, 128)


def image_norm_kernel(place, *refs):
    *images, gain, out = refs
    for k, part in enumerate(images):
        rows = part.shape[0]
        at = pl.multiple_of((place[0] ^ k) * rows, rows)
        out[pl.ds(at, rows), :] = normed(part[...], gain[...])


def attend(reduced, kept, values_t, bias, out_t, lse, head):
    for at in range(0, kept.shape[0], CHUNK):
        scores = dot_nt(reduced, kept[at : at + CHUNK])
        if bias is not None:
            scores = scores + bias
        top = jnp.max(scores, axis=0, keepdims=True)
        weights = jnp.exp2(scores - top)
        total = jnp.sum(weights, axis=0, keepdims=True)
        numer = dot(values_t, weights.astype(BF))
        out_t[:, at : at + CHUNK] = (numer * (1.0 / total)).astype(BF)
        stat = top + jnp.log2(total)
        rows = kept.shape[0] // 128
        for k in range(CHUNK // 128):
            lse[pl.ds(head * rows + at // 128 + k, 1), :] = stat[:, k * 128 : (k + 1) * 128]


def copied_at_end(head, lse, lse_copies):
    @pl.when(head == pl.num_programs(0) - 1)
    def _():
        lse_copies[...] = jnp.broadcast_to(lse[...][None], lse_copies.shape)


def queries_of(images, query_w):
    factor = math.log2(math.e) / math.sqrt(HD)
    return (dot(images[...], query_w[...]) * factor).astype(BF)


def column_kernel(
    images, packed, gain, query_w, value_w, key_w, out_t, lse, lse_copies, held
):
    head = pl.program_id(0)

    @pl.when(head == 0)
    def _():
        held[...] = normed(tokens_of(packed), gain[...])

    values_t = dot_nt(value_w[...].T, images[...]).astype(BF)
    key = dot(held[...], key_w[...]).astype(BF)
    attend(queries_of(images, query_w), key, values_t, None, out_t, lse, head)
    copied_at_end(head, lse, lse_copies)


def row_kernel(
    images, packed, gain, query_w, key_w, value_w, out_t, lse, members, held, bias
):
    head = pl.program_id(0)

    @pl.when(head == 0)
    def _():
        held[...] = normed(tokens_of(packed), gain[...])
        codes = codes_of(packed)
        members[...] = members_of(codes, 0, members.shape[0]).astype(BF)
        bias[...] = jnp.broadcast_to(jnp.where(codes[:, :1] > 0, 0.0, MASKED), bias.shape)

    values_t = dot_nt(value_w[...].T, held[...]).astype(BF)
    key = dot(held[...], key_w[...]).astype(BF)
    attend(key, queries_of(images, query_w), values_t, bias[:, :1], out_t, lse, head)


def add_projected(share, out_t, out_w, total):
    head = pl.program_id(0)
    rows = share.shape[0] // pl.num_programs(0)
    line = jnp.concatenate([share[pl.ds(head * rows + k, 1), :] for k in range(rows)], axis=1)
    term = dot(out_w[...].T, (out_t[...] * line).astype(BF))

    @pl.when(head == 0)
    def _():
        total[...] = term

    @pl.when(head > 0)
    def _():
        total[...] += term


def image_out_kernel(place, lse_whole, lse, out_t, out_w, *refs):
    *sent, share, total, turned = refs
    head = pl.program_id(0)

    @pl.when(head == 0)
    def _():
        share[...] = jnp.exp2(lse[...] - lse_whole[...])

    add_projected(share, out_t, out_w, total)

    @pl.when(head == pl.num_programs(0) - 1)
    def _():
        turned[...] = total[...].T.astype(BF)
        for k, part in enumerate(sent):
            rows = part.shape[0]
            part[...] = turned[pl.ds(pl.multiple_of((place[0] ^ k) * rows, rows), rows), :]


def members_of(codes, first, count):
    lines = codes.T
    ids = lines[1:2] * 16.0 + lines[2:3]
    wanted = (first + lax.broadcasted_iota(jnp.int32, (count, codes.shape[0]), 0)).astype(F32)
    return jnp.where(ids == wanted, jnp.where(lines[0:1] > 0, 1.0, 0.0), 0.0)


def prompt_out_kernel(lse_all, lse, out_t, out_w, members, sent, share, total, held):
    head = pl.program_id(0)

    @pl.when(head == 0)
    def _():
        gathered = lse_all[...]
        highest = jnp.max(gathered, axis=0)
        summed = jnp.sum(jnp.exp2(gathered - highest[None]), axis=0)
        share[...] = jnp.exp2(lse[...] - highest - jnp.log2(summed))

    held[pl.ds(head * members.shape[0], members.shape[0]), :] = members[...]
    add_projected(share, out_t, out_w, total)

    @pl.when(head == pl.num_programs(0) - 1)
    def _():
        contribution = total[...].T.astype(BF)
        peers, rows, wide = sent.shape
        depth = wide - 128
        sent[:, :, :depth] = contribution.reshape(peers, rows, depth)
        sums = dot(held[...], contribution).astype(BF)
        for group in range(peers // 2):
            for side in range(2):
                sent[2 * group + side, :, depth:] = sums[
                    group * rows : (group + 1) * rows, side * 128 : (side + 1) * 128
                ]


def category_kernel(place, arrived, packed, scale, out):
    _, rows, wide = arrived.shape
    depth = wide - 128
    group, side = place[0] // 2, place[0] % 2
    members = members_of(codes_of(packed), group * rows, rows)
    base = dot(members.astype(BF), tokens_of(packed))
    own = jnp.where(side == 0, base[:, :128], base[:, 128:])
    factor = jnp.where(side == 0, scale[:, :128], scale[:, 128:])
    sums = own + factor * jnp.sum(arrived[:, :, depth:].astype(F32), axis=0)
    tally = jnp.broadcast_to(jnp.sum(members, axis=1, keepdims=True), sums.shape)
    out[:, :, :128] = jnp.broadcast_to(sums[None], (out.shape[0], rows, 128))
    out[:, :, 128:] = jnp.broadcast_to(tally[None], (out.shape[0], rows, 128))


def mean_kernel(partials, out):
    sums = jnp.sum(partials[...], axis=0)
    out[...] = jnp.broadcast_to((sums[:, :128] / sums[:, 128:]).astype(BF)[None], out.shape)


def table_kernel(pieces, out):
    rows = pieces.shape[1]
    for group in range(pieces.shape[0] // 2):
        for side in range(2):
            out[group * rows : (group + 1) * rows, side * 128 : (side + 1) * 128] = pieces[
                2 * group + side
            ].astype(F32)


def block(shape, index):
    return pl.BlockSpec(shape, index)


def whole(array):
    rank = len(array.shape)
    return pl.BlockSpec(array.shape, lambda h: (0,) * rank)


def shaped(shape, dtype):
    return jax.ShapeDtypeStruct(shape, dtype)


def far(shape, dtype):
    return pltpu.HBM(shape, dtype)


def kept_far(*arrays):
    return [pltpu.with_memory_space_constraint(a, pltpu.HBM) for a in arrays]


def cost(flops, moved, exps=0):
    return pl.CostEstimate(flops=flops, bytes_accessed=moved, transcendentals=exps)


LIMIT = 16 * 2**20


def params(**more):
    return pltpu.CompilerParams(vmem_limit_bytes=LIMIT, **more)


def on_device(
    image_tokens,
    prompt_tokens,
    category_ids,
    prompt_valid,
    image_gain,
    prompt_gain,
    query_weight,
    key_weight,
    image_value_weight,
    prompt_value_weight,
    image_out_weight,
    prompt_out_weight,
    image_layer_scale,
    prompt_layer_scale,
):
    width = query_weight.shape[1]
    heads = width // HD
    depth = image_tokens.shape[1]
    planes = lax.axis_size(PLANE)
    columns = lax.axis_size(COLUMN)
    own_prompts = prompt_tokens.shape[0]
    own_images = image_tokens.shape[0]
    images = own_images * columns
    prompts = own_prompts * planes
    categories = prompts * columns // 16

    packed = pl.pallas_call(
        pack_kernel,
        out_shape=shaped((planes, 2 * own_prompts + 8, 128), BF),
        compiler_params=params(),
        name="pack",
    )(*kept_far(prompt_tokens, category_ids.reshape(1, -1), prompt_valid.reshape(1, -1)))
    prompt_all = swap(packed, PLANE)
    image_parts = [image_tokens]
    for k in range(1, columns):
        turned = [(i, i ^ k) for i in range(columns)]
        image_parts.append(lax.ppermute(image_tokens, COLUMN, turned))

    head_columns = lambda n: block((n, HD), lambda h: (0, h))
    head_rows = lambda n: block((HD, n), lambda h: (h, 0))
    row = lambda n: block((1, n), lambda h: (0, 0))

    pair_flops = 4 * images * prompts * width
    stat_rows = heads * prompts // 128
    stats = lambda n: block((n, 128), lambda h: (0, 0))
    scalar = pl.BlockSpec(memory_space=pltpu.SMEM)
    column_place = lax.axis_index(COLUMN).astype(jnp.int32).reshape(1)
    image_row = image_gain.reshape(1, depth)
    prompt_row = prompt_gain.reshape(1, depth)
    image_normed = pl.pallas_call(
        image_norm_kernel,
        in_specs=[scalar] + [pl.BlockSpec(memory_space=pltpu.VMEM)] * (columns + 1),
        out_shape=shaped((images, depth), BF),
        compiler_params=params(),
        cost_estimate=cost(10 * images * depth, 4 * images * depth),
        name="image_norm",
    )(column_place, *kept_far(image_tokens), *image_parts[1:], *kept_far(image_row))
    prompt_part_t, col_lse, col_lse_copies = pl.pallas_call(
        column_kernel,
        grid=(heads,),
        in_specs=[
            whole(image_normed),
            whole(prompt_all),
            row(depth),
            head_columns(depth),
            head_columns(depth),
            head_columns(depth),
        ],
        out_specs=[
            head_rows(prompts),
            stats(stat_rows),
            block((planes, stat_rows, 128), lambda h: (0, 0, 0)),
        ],
        out_shape=[
            far((width, prompts), BF),
            shaped((stat_rows, 128), F32),
            shaped((planes, stat_rows, 128), F32),
        ],
        scratch_shapes=[pltpu.VMEM((prompts, depth), BF)],
        compiler_params=params(dimension_semantics=("arbitrary",)),
        cost_estimate=cost(2 * pair_flops, 6 * images * width, images * prompts * heads),
        name="column_attention",
    )(image_normed, prompt_all, *kept_far(prompt_row, query_weight, image_value_weight, key_weight))

    col_lse_all = swap(col_lse_copies, PLANE)

    row_stat_rows = heads * images // 128
    image_part_t, row_lse, members = pl.pallas_call(
        row_kernel,
        grid=(heads,),
        in_specs=[
            whole(image_normed),
            whole(prompt_all),
            row(depth),
            head_columns(depth),
            head_columns(depth),
            head_columns(depth),
        ],
        out_specs=[
            head_rows(images),
            stats(row_stat_rows),
            block((categories, prompts), lambda h: (0, 0)),
        ],
        out_shape=[
            far((width, images), BF),
            shaped((row_stat_rows, 128), F32),
            far((categories, prompts), BF),
        ],
        scratch_shapes=[pltpu.VMEM((prompts, depth), BF), pltpu.VMEM((prompts, 128), F32)],
        compiler_params=params(dimension_semantics=("arbitrary",)),
        cost_estimate=cost(2 * pair_flops, 6 * images * width, images * prompts * heads),
        name="row_attention",
    )(
        image_normed,
        prompt_all,
        *kept_far(prompt_row, query_weight, key_weight, prompt_value_weight),
    )

    row_whole = row_lse
    for bit in (1, 2, 4):
        other = lax.ppermute(row_whole, COLUMN, [(i, i ^ bit) for i in range(columns)])
        apart = jnp.exp2(-jnp.abs(row_whole - other))
        row_whole = jnp.maximum(row_whole, other) + jnp.log2(1.0 + apart)

    plane_sent = pl.pallas_call(
        prompt_out_kernel,
        grid=(heads,),
        in_specs=[
            whole(col_lse_all),
            whole(col_lse),
            head_rows(prompts),
            head_rows(depth),
            block((categories // heads, prompts), lambda h: (h, 0)),
        ],
        out_specs=block((planes, own_prompts, depth + 128), lambda h: (0, 0, 0)),
        out_shape=shaped((planes, own_prompts, depth + 128), BF),
        scratch_shapes=[
            pltpu.VMEM(col_lse.shape, F32),
            pltpu.VMEM((depth, prompts), F32),
            pltpu.VMEM((categories, prompts), BF),
        ],
        compiler_params=params(dimension_semantics=("arbitrary",)),
        cost_estimate=cost(2 * prompts * depth * (width + categories), 6 * prompts * width),
        name="prompt_projection_out",
    )(col_lse_all, col_lse, *kept_far(prompt_part_t, prompt_out_weight, members))
    plane_arrived = swap(plane_sent, PLANE)

    image_sent = pl.pallas_call(
        image_out_kernel,
        grid=(heads,),
        in_specs=[scalar, whole(row_whole), whole(row_lse), head_rows(images), head_rows(depth)],
        out_specs=[block((own_images, depth), lambda h: (0, 0))] * columns,
        out_shape=[shaped((own_images, depth), BF)] * columns,
        scratch_shapes=[
            pltpu.VMEM(row_lse.shape, F32),
            pltpu.VMEM((depth, images), F32),
            pltpu.VMEM((images, depth), BF),
        ],
        compiler_params=params(dimension_semantics=("arbitrary",)),
        cost_estimate=cost(2 * images * depth * width, 6 * images * width),
        name="image_projection_out",
    )(column_place, row_whole, row_lse, *kept_far(image_part_t, image_out_weight))

    category_copies = pl.pallas_call(
        category_kernel,
        in_specs=[scalar] + [pl.BlockSpec(memory_space=pltpu.VMEM)] * 3,
        out_shape=shaped((columns, own_prompts, depth), F32),
        compiler_params=params(),
        cost_estimate=cost(2 * own_prompts * prompts * depth, 4 * prompts * depth),
        name="category_partial",
    )(
        lax.axis_index(PLANE).astype(jnp.int32).reshape(1),
        plane_arrived,
        prompt_all,
        prompt_layer_scale.reshape(1, depth),
    )
    partials = swap(category_copies, COLUMN)
    mean_copies = pl.pallas_call(
        mean_kernel,
        out_shape=shaped((planes, own_prompts, 128), BF),
        compiler_params=params(),
        name="category_mean",
    )(partials)
    mean_all = swap(mean_copies, PLANE)
    category_embed = pl.pallas_call(
        table_kernel,
        out_shape=shaped((categories, depth), F32),
        compiler_params=params(),
        name="category_table",
    )(mean_all)

    image_delta = image_sent[0].astype(F32)
    for k in range(1, columns):
        turned = [(i, i ^ k) for i in range(columns)]
        image_delta += lax.ppermute(image_sent[k], COLUMN, turned).astype(F32)
    joined_image = (image_tokens.astype(F32) + image_layer_scale * image_delta).astype(BF)
    prompt_delta = jnp.sum(plane_arrived[:, :, :depth].astype(F32), axis=0)
    joined_prompt = (prompt_tokens.astype(F32) + prompt_layer_scale * prompt_delta).astype(BF)
    return (joined_image, joined_prompt, category_embed)


def solution(mesh):
    finer = Mesh(mesh.devices.reshape(4, 8, 2, 2, 2), ALL)
    replicated = (P(),) * 10
    return jax.shard_map(
        on_device,
        mesh=finer,
        in_specs=(P(ALL, None), P(PROMPT_ORDER, None), P(PROMPT_ORDER), P(PROMPT_ORDER), *replicated),
        out_specs=(P(ALL, None), P(PROMPT_ORDER, None), P()),
        check_vma=False,
    )
```

time: 188 us -> 128 us (0.68)
  local copies, waits for them, and re-layouts: 37.8 us -> 0.01 us
  blocking collectives: 24.7 us -> 0 us
  Pallas kernels: 22.8 us -> 34.5 us
  waiting for transfers between devices: 34.5 us -> 28.2 us
    unnamed x69 -> x8, local copies, waits for them, and re-layouts: 27.4 us -> 0.01 us
    all_to_all x2 -> x0, blocking collectives: 24.7 us -> none  [swap(): return lax.all_to_all(parts, axes, split_axis=0, concat_axis=0, tiled=True)]
    all_to_all x8 -> x5, starting transfers between devices: 62.5 us -> 41.1 us  [swap(): return lax.all_to_all(parts, axes, split_axis=0, concat_axis=0, tiled=True)]
    ppermute x0 -> x17, starting transfers between devices: none -> 21.1 us  [the longest x7 10.1 us: on_device(): image_parts.append(lax.ppermute(image_tokens, COLUMN, turned))]
    all_to_all x8 -> x5, waiting for transfers between devices: 34.5 us -> 16.2 us  [swap(): return lax.all_to_all(parts, axes, split_axis=0, concat_axis=0, tiled=True)]
    ppermute x0 -> x17, waiting for transfers between devices: none -> 11.9 us  [the longest x3 7.38 us: on_device(): lax.ppermute(row_whole, COLUMN, [(i, i ^ bit) for i in range(columns)])]
    pallas_call x6 -> x9, Pallas kernels: 22.8 us -> 34.5 us  [the longest x1 10.3 us: on_device(): pl.pallas_call(column_kernel, grid=(heads,), in_specs=[whole(image_normed...]
    broadcast_in_dim x7 -> x0, local copies, waits for them, and re-layouts: 5.28 us -> none  [spread(): copies = jnp.broadcast_to(shard, (lax.axis_size(axes), *shard.shape))]
  transfers between devices with their start and end apart: 8 -> 22, of which waited for: 5 -> 9; matrix products, arithmetic and copies ran while one was open for 7% -> 1% of each run, Pallas kernels for 12% -> 13%
where the time goes in v2:
time: 128 us; the launch traced here: 127 us
  starting transfers between devices  62.2 us (49%)
  Pallas kernels  34.5 us (27%)
  waiting for transfers between devices  28.2 us (22%)
  other arithmetic  1.45 us (1%)
    all_to_all x5, starting transfers between devices, swap(): return lax.all_to_all(parts, axes, split_axis=0, concat_axis=0, tiled=True)  41.1 us
    all_to_all x5, waiting for transfers between devices, swap(): return lax.all_to_all(parts, axes, split_axis=0, concat_axis=0, tiled=True)  16.2 us
    pallas_call x1, Pallas kernels, on_device(): pl.pallas_call(column_kernel, grid=(heads,), in_specs=[whole(image_normed...  10.3 us
    pallas_call x1, Pallas kernels, on_device(): pl.pallas_call(row_kernel, grid=(heads,), in_specs=[whole(image_normed),...  10.3 us
    ppermute x7, starting transfers between devices, on_device(): image_parts.append(lax.ppermute(image_tokens, COLUMN, turned))  10.1 us
    ppermute x7, starting transfers between devices, on_device(): image_delta += lax.ppermute(image_sent[k], COLUMN, turned).astype(F32)  8.97 us
    ppermute x3, waiting for transfers between devices, on_device(): lax.ppermute(row_whole, COLUMN, [(i, i ^ bit) for i in range(columns)])  7.38 us
    pallas_call x1, Pallas kernels, on_device(): pl.pallas_call(prompt_out_kernel, grid=(heads,), in_specs=[whole(col_lse_...  4.7 us
  transfers between devices with their start and end apart: 22, of which 9 were waited for; matrix products, arithmetic and copies ran while one was open for 1% of the time, Pallas kernels for 13%

profile of v2, /device:TPU:1, one launch (start us, length us, event | category | flops | bytes accessed | tf_op | source)
XLA Modules:
  0.0 127.1 jit_solution(368677124304252484)
XLA Ops:
  0.6 1.6 %pack.1 = bf16[32,56,128]{2,1,0:T(8,128)(2,1)} custom-call(bf16[24,256]{1,0:T(8,128)(2,1)} %tokens.1, s32[1,24]{1,0:T(1,128)} %bitcast.9, s32[1,24]{1,0:T(1,128)} %bitcast.10), custom_call_target="tpu_custom_call" | custom-call | tf_op jit(solution)/shard_map/pack/pallas_call | solution.py:303
  2.2 11.9 %all-to-all-start = ((bf16[32,56,128]{2,1,0:T(8,128)(2,1)}), bf16[32,56,128]{2,1,0:T(8,128)(2,1)S(1)}, u32[]{:S(2)}, u32[]{:S(2)}) async-start(bf16[32,56,128]{2,1,0:T(8,128)(2,1)} %pack.1), calls=%async_computation | async-start | bytes 917504 | tf_op jit(solution)/shard_map/all_to_all | solution.py:25
  14.1 1.0 collective-permute-start
  15.1 2.9 %collective-permute-start.1 = (bf16[128,256]{1,0:T(8,128)(2,1)}, bf16[128,256]{1,0:T(8,128)(2,1)S(1)}, u32[]{:S(2)}, u32[]{:S(2)}) collective-permute-start(bf16[128,256]{1,0:T(8,128)(2,1)} %refs_0_.1), channel_id=1, source_target_pairs={{0,2},{1,3},{2,0},{3,1},{4,6},{5,7},{6,4},{7,5},{8,10},{9,11},{10,... | collective-permute-start | bytes 196616 | tf_op jit(solution)/shard_map/ppermute | solution.py:313
  18.0 0.3 collective-permute-start.2
  18.4 1.3 %collective-permute-start.3 = (bf16[128,256]{1,0:T(8,128)(2,1)}, bf16[128,256]{1,0:T(8,128)(2,1)S(1)}, u32[]{:S(2)}, u32[]{:S(2)}) collective-permute-start(bf16[128,256]{1,0:T(8,128)(2,1)} %refs_0_.1), channel_id=1, source_target_pairs={{0,4},{1,5},{2,6},{3,7},{4,0},{5,1},{6,2},{7,3},{8,12},{9,13},{10,... | collective-permute-start | bytes 196616 | tf_op jit(solution)/shard_map/ppermute | solution.py:313
  19.7 0.5 collective-permute-start.4
  20.1 0.0 collective-permute-done.refs_1_
  20.1 2.7 %collective-permute-start.5 = (bf16[128,256]{1,0:T(8,128)(2,1)}, bf16[128,256]{1,0:T(8,128)(2,1)S(1)}, u32[]{:S(2)}, u32[]{:S(2)}) collective-permute-start(bf16[128,256]{1,0:T(8,128)(2,1)} %refs_0_.1), channel_id=1, source_target_pairs={{0,6},{1,7},{2,4},{3,5},{4,2},{5,3},{6,0},{7,1},{8,14},{9,15},{10,... | collective-permute-start | bytes 196616 | tf_op jit(solution)/shard_map/ppermute | solution.py:313
  22.9 0.0 collective-permute-done.1.refs_2_
  22.9 1.3 %collective-permute-start.6 = (bf16[128,256]{1,0:T(8,128)(2,1)}, bf16[128,256]{1,0:T(8,128)(2,1)S(1)}, u32[]{:S(2)}, u32[]{:S(2)}) collective-permute-start(bf16[128,256]{1,0:T(8,128)(2,1)} %refs_0_.1), channel_id=1, source_target_pairs={{0,7},{1,6},{2,5},{3,4},{4,3},{5,2},{6,1},{7,0},{8,15},{9,14},{10,... | collective-permute-start | bytes 196616 | tf_op jit(solution)/shard_map/ppermute | solution.py:313
  24.2 0.3 collective-permute-done.2.refs_3_
  24.4 0.0 collective-permute-done.3.refs_4_
  24.4 1.1 collective-permute-done.4.refs_5_
  25.5 0.0 collective-permute-done.5.refs_6_
  25.5 3.2 %collective-permute-done.6.refs_7_ = bf16[128,256]{1,0:T(8,128)(2,1)S(1)} collective-permute-done((bf16[128,256]{1,0:T(8,128)(2,1)}, bf16[128,256]{1,0:T(8,128)(2,1)S(1)}, u32[]{:S(2)}, u32[]{:S(2)}) %collective-permute-start.6) | collective-permute-done | bytes 65568 | tf_op jit(solution)/shard_map/ppermute | solution.py:313
  28.7 1.4 %image_norm.1.images = bf16[1024,256]{1,0:T(8,128)(2,1)S(1)} custom-call(s32[1]{0:T(128)} %bitcast.place, bf16[128,256]{1,0:T(8,128)(2,1)} %refs_0_.1, bf16[128,256]{1,0:T(8,128)(2,1)S(1)} %collective-permute-done.refs_1_, bf16[128,256]{1,0:T(8,128)(2,1)S(1)} %collective-permute-done.1.refs_2_, bf16[128,256]{1,0:T(8,128)(2,1)S(1)} %collective-permute-done.2.refs_3_, ...), custom_call_target="tpu_custom_call" | custom-call | flops 2621440 | bytes 1048576 | tf_op jit(solution)/shard_map/image_norm/pallas_call | solution.py:326
  30.1 0.0 all-to-all-done.packed
  30.1 10.3 %column_attention.1 = (bf16[1024,768]{1,0:T(8,128)(2,1)}, f32[24,128]{1,0:T(8,128)S(1)}, f32[32,24,128]{2,1,0:T(8,128)}) custom-call(bf16[1024,256]{1,0:T(8,128)(2,1)S(1)} %image_norm.1.images, bf16[32,56,128]{2,1,0:T(8,128)(2,1)S(1)} %all-to-all-done.packed, f32[1,256]{1,0:T(1,128)} %bitcast.11, bf16[256,1024]{1,0:T(8,128)(2,1)} %query_w.3, ...), custom_call_target="tpu_custom_call" | custom-call | flops 6442450944 | bytes 6291456 | tf_op jit(solution)/shard_map/column_attention/pallas_call | solution.py:334
  40.4 9.2 %all-to-all-start.1 = ((f32[32,24,128]{2,1,0:T(8,128)}), f32[32,24,128]{2,1,0:T(8,128)S(1)}, u32[]{:S(2)}, u32[]{:S(2)}) async-start(f32[32,24,128]{2,1,0:T(8,128)} %get-tuple-element.27), calls=%async_computation.1 | async-start | bytes 786432 | tf_op jit(solution)/shard_map/all_to_all | solution.py:25
  49.6 10.3 %row_attention.1 = (bf16[1024,1024]{1,0:T(8,128)(2,1)}, f32[32,128]{1,0:T(8,128)S(1)}, bf16[384,768]{1,0:T(8,128)(2,1)}) custom-call(bf16[1024,256]{1,0:T(8,128)(2,1)S(1)} %image_norm.1.images, bf16[32,56,128]{2,1,0:T(8,128)(2,1)S(1)} %all-to-all-done.packed, f32[1,256]{1,0:T(1,128)} %bitcast.12, bf16[256,1024]{1,0:T(8,128)(2,1)} %query_w.3, ...), custom_call_target="tpu_custom_call" | custom-call | flops 6442450944 | bytes 6291456 | tf_op jit(solution)/shard_map/row_attention/pallas_call | solution.py:364
  59.9 1.5 %all-to-all-done.1.lse_all = f32[32,24,128]{2,1,0:T(8,128)S(1)} async-done(((f32[32,24,128]{2,1,0:T(8,128)}), f32[32,24,128]{2,1,0:T(8,128)S(1)}, u32[]{:S(2)}, u32[]{:S(2)}) %all-to-all-start.1) | async-done | bytes 393248 | tf_op jit(solution)/shard_map/all_to_all | solution.py:25
  61.4 0.0 copy-start
  61.4 4.7 %prompt_projection_out.1 = bf16[32,24,384]{2,1,0:T(8,128)(2,1)} custom-call(f32[32,24,128]{2,1,0:T(8,128)S(1)} %all-to-all-done.1.lse_all, f32[24,128]{1,0:T(8,128)S(1)} %get-tuple-element.28.lse, bf16[1024,768]{1,0:T(8,128)(2,1)} %get-tuple-element.29.out_t, bf16[1024,256]{1,0:T(8,128)(2,1)} %out_w.3, bf16[384,768]{1,0:T(8,128)(2,1)} %get-tuple-element.30.members), custom_call_target="tpu_custom_call" | custom-call | flops 553648128 | bytes 4718592 | tf_op jit(solution)/shard_map/prompt_projection_out/pallas_call | solution.py:401
  66.1 7.7 %all-to-all-start.2 = ((bf16[32,24,384]{2,1,0:T(8,128)(2,1)}), bf16[32,24,384]{2,1,0:T(8,128)(2,1)S(1)}, u32[]{:S(2)}, u32[]{:S(2)}) async-start(bf16[32,24,384]{2,1,0:T(8,128)(2,1)} %prompt_projection_out.1), calls=%async_computation.2 | async-start | bytes 1179648 | tf_op jit(solution)/shard_map/all_to_all | solution.py:25
  73.8 1.3 %collective-permute-start.7 = (f32[32,128]{1,0:T(8,128)S(1)}, f32[32,128]{1,0:T(8,128)S(1)}, u32[]{:S(2)}, u32[]{:S(2)}) collective-permute-start(f32[32,128]{1,0:T(8,128)S(1)} %get-tuple-element.17.lse), channel_id=1, source_target_pairs={{0,1},{1,0},{2,3},{3,2},{4,5},{5,4},{6,7},{7,6},{8,9},{9,8},{10,11... | collective-permute-start | bytes 49160 | tf_op jit(solution)/shard_map/ppermute | solution.py:397
  75.2 0.8 collective-permute-done.7
  76.0 0.7 collective-permute-start.8
  76.7 3.7 %collective-permute-done.8 = f32[32,128]{1,0:T(8,128)S(1)} collective-permute-done((f32[32,128]{1,0:T(8,128)S(1)}, f32[32,128]{1,0:T(8,128)S(1)}, u32[]{:S(2)}, u32[]{:S(2)}) %collective-permute-start.8) | collective-permute-done | bytes 16416 | tf_op jit(solution)/shard_map/ppermute | solution.py:397
  80.4 0.1 collective-permute-start.9
  80.5 2.9 %collective-permute-done.9 = f32[32,128]{1,0:T(8,128)S(1)} collective-permute-done((f32[32,128]{1,0:T(8,128)S(1)}, f32[32,128]{1,0:T(8,128)S(1)}, u32[]{:S(2)}, u32[]{:S(2)}) %collective-permute-start.9) | collective-permute-done | bytes 16416 | tf_op jit(solution)/shard_map/ppermute | solution.py:397
  83.4 6.1 %all-to-all-done.2.arrived = bf16[32,24,384]{2,1,0:T(8,128)(2,1)S(1)} async-done(((bf16[32,24,384]{2,1,0:T(8,128)(2,1)}), bf16[32,24,384]{2,1,0:T(8,128)(2,1)S(1)}, u32[]{:S(2)}, u32[]{:S(2)}) %all-to-all-start.2) | async-done | bytes 589856 | tf_op jit(solution)/shard_map/all_to_all | solution.py:25
  89.5 0.0 copy-done
  89.5 1.0 category_partial.1
  90.5 0.0 copy-start.1
  90.5 0.0 copy-start.3
  90.5 7.2 %all-to-all-start.3 = ((f32[8,24,256]{2,1,0:T(8,128)}), f32[8,24,256]{2,1,0:T(8,128)S(1)}, u32[]{:S(2)}, u32[]{:S(2)}) async-start(f32[8,24,256]{2,1,0:T(8,128)} %category_partial.1), calls=%async_computation.3 | async-start | bytes 393216 | tf_op jit(solution)/shard_map/all_to_all | solution.py:25
  97.7 0.0 copy-start.2
  97.7 3.7 %image_projection_out.1 = (bf16[128,256]{1,0:T(8,128)(2,1)S(1)}, bf16[128,256]{1,0:T(8,128)(2,1)S(1)}, bf16[128,256]{1,0:T(8,128)(2,1)S(1)}, bf16[128,256]{1,0:T...) custom-call(s32[1]{0:T(128)} %bitcast.place, ...), custom_call_target="tpu_custom_call" | custom-call | flops 536870912 | bytes 6291456 | tf_op jit(solution)/shard_map/image_projection_out/pallas_call | solution.py:424
  101.4 0.2 collective-permute-start.10
  101.6 3.1 %collective-permute-start.11 = (bf16[128,256]{1,0:T(8,128)(2,1)S(1)}, bf16[128,256]{1,0:T(8,128)(2,1)S(1)}, u32[]{:S(2)}, u32[]{:S(2)}) collective-permute-start(bf16[128,256]{1,0:T(8,128)(2,1)S(1)} %get-tuple-element.21), channel_id=1, source_target_pairs={{0,2},{1,3},{2,0},{3,1},{4,6},{5,7},{6,4},{7,5},{8,10},{9,11},{10,... | collective-permute-start | bytes 196616 | tf_op jit(solution)/shard_map/ppermute | solution.py:471
  104.7 0.4 collective-permute-start.12
  105.1 1.4 %collective-permute-start.13 = (bf16[128,256]{1,0:T(8,128)(2,1)S(1)}, bf16[128,256]{1,0:T(8,128)(2,1)S(1)}, u32[]{:S(2)}, u32[]{:S(2)}) collective-permute-start(bf16[128,256]{1,0:T(8,128)(2,1)S(1)} %get-tuple-element.23), channel_id=1, source_target_pairs={{0,4},{1,5},{2,6},{3,7},{4,0},{5,1},{6,2},{7,3},{8,12},{9,13},{10,... | collective-permute-start | bytes 196616 | tf_op jit(solution)/shard_map/ppermute | solution.py:471
  106.5 0.3 collective-permute-start.14
  106.8 0.0 collective-permute-done.10
  106.8 2.7 %collective-permute-start.15 = (bf16[128,256]{1,0:T(8,128)(2,1)S(1)}, bf16[128,256]{1,0:T(8,128)(2,1)S(1)}, u32[]{:S(2)}, u32[]{:S(2)}) collective-permute-start(bf16[128,256]{1,0:T(8,128)(2,1)S(1)} %get-tuple-element.25), channel_id=1, source_target_pairs={{0,6},{1,7},{2,4},{3,5},{4,2},{5,3},{6,0},{7,1},{8,14},{9,15},{10,... | collective-permute-start | bytes 196616 | tf_op jit(solution)/shard_map/ppermute | solution.py:471
  109.5 0.0 collective-permute-done.11
  109.5 0.9 collective-permute-start.16
  110.4 0.0 all-to-all-done.3.partials
  110.4 0.7 category_mean.1
  111.1 5.1 %all-to-all-start.4 = ((bf16[32,24,128]{2,1,0:T(8,128)(2,1)}), bf16[32,24,128]{2,1,0:T(8,128)(2,1)S(1)}, u32[]{:S(2)}, u32[]{:S(2)}) async-start(bf16[32,24,128]{2,1,0:T(8,128)(2,1)} %category_mean.1), calls=%async_computation.4 | async-start | bytes 393216 | tf_op jit(solution)/shard_map/all_to_all | solution.py:25
  116.2 0.0 collective-permute-done.12
  116.3 0.0 collective-permute-done.13
  116.3 0.0 collective-permute-done.14
  116.3 0.0 collective-permute-done.15
  116.3 0.0 collective-permute-done.16
  116.3 0.0 copy-done.1
  116.3 0.0 copy-done.3
  116.3 0.7 add_convert_fusion
  117.0 0.1 convert_reduce_fusion
  117.1 0.0 copy-done.2
  117.1 0.6 add_convert_fusion.1
  117.7 8.6 %all-to-all-done.4.pieces = bf16[32,24,128]{2,1,0:T(8,128)(2,1)S(1)} async-done(((bf16[32,24,128]{2,1,0:T(8,128)(2,1)}), bf16[32,24,128]{2,1,0:T(8,128)(2,1)S(1)}, u32[]{:S(2)}, u32[]{:S(2)}) %all-to-all-start.4) | async-done | bytes 196640 | tf_op jit(solution)/shard_map/all_to_all | solution.py:25
  126.3 0.8 category_table.1
  (3 shorter events, 0.1 us)
Async XLA Ops:
  2.2 27.9 %all-to-all-start = ((bf16[32,56,128]{2,1,0:T(8,128)(2,1)}), bf16[32,56,128]{2,1,0:T(8,128)(2,1)S(1)}, u32[]{:S(2)}, u32[]{:S(2)}) async-start(bf16[32,56,128]{2,1,0:T(8,128)(2,1)} %pack.1), calls=%async_computation | async-start | bytes 917504 | tf_op jit(solution)/shard_map/all_to_all | solution.py:25
  14.1 6.0 %collective-permute-start = (bf16[128,256]{1,0:T(8,128)(2,1)}, bf16[128,256]{1,0:T(8,128)(2,1)S(1)}, u32[]{:S(2)}, u32[]{:S(2)}) collective-permute-start(bf16[128,256]{1,0:T(8,128)(2,1)} %refs_0_.1), channel_id=1, source_target_pairs={{0,1},{1,0},{2,3},{3,2},{4,5},{5,4},{6,7},{7,6},{8,9},{9,8},{10,11... | collective-permute-start | bytes 196616 | tf_op jit(solution)/shard_map/ppermute | solution.py:313
  15.1 7.7 %collective-permute-start.1 = (bf16[128,256]{1,0:T(8,128)(2,1)}, bf16[128,256]{1,0:T(8,128)(2,1)S(1)}, u32[]{:S(2)}, u32[]{:S(2)}) collective-permute-start(bf16[128,256]{1,0:T(8,128)(2,1)} %refs_0_.1), channel_id=1, source_target_pairs={{0,2},{1,3},{2,0},{3,1},{4,6},{5,7},{6,4},{7,5},{8,10},{9,11},{10,... | collective-permute-start | bytes 196616 | tf_op jit(solution)/shard_map/ppermute | solution.py:313
  18.0 6.4 %collective-permute-start.2 = (bf16[128,256]{1,0:T(8,128)(2,1)}, bf16[128,256]{1,0:T(8,128)(2,1)S(1)}, u32[]{:S(2)}, u32[]{:S(2)}) collective-permute-start(bf16[128,256]{1,0:T(8,128)(2,1)} %refs_0_.1), channel_id=1, source_target_pairs={{0,3},{1,2},{2,1},{3,0},{4,7},{5,6},{6,5},{7,4},{8,11},{9,10},{10,... | collective-permute-start | bytes 196616 | tf_op jit(solution)/shard_map/ppermute | solution.py:313
  18.4 6.1 %collective-permute-start.3 = (bf16[128,256]{1,0:T(8,128)(2,1)}, bf16[128,256]{1,0:T(8,128)(2,1)S(1)}, u32[]{:S(2)}, u32[]{:S(2)}) collective-permute-start(bf16[128,256]{1,0:T(8,128)(2,1)} %refs_0_.1), channel_id=1, source_target_pairs={{0,4},{1,5},{2,6},{3,7},{4,0},{5,1},{6,2},{7,3},{8,12},{9,13},{10,... | collective-permute-start | bytes 196616 | tf_op jit(solution)/shard_map/ppermute | solution.py:313
  19.7 5.8 %collective-permute-start.4 = (bf16[128,256]{1,0:T(8,128)(2,1)}, bf16[128,256]{1,0:T(8,128)(2,1)S(1)}, u32[]{:S(2)}, u32[]{:S(2)}) collective-permute-start(bf16[128,256]{1,0:T(8,128)(2,1)} %refs_0_.1), channel_id=1, source_target_pairs={{0,5},{1,4},{2,7},{3,6},{4,1},{5,0},{6,3},{7,2},{8,13},{9,12},{10,... | collective-permute-start | bytes 196616 | tf_op jit(solution)/shard_map/ppermute | solution.py:313
  20.1 5.4 %collective-permute-start.5 = (bf16[128,256]{1,0:T(8,128)(2,1)}, bf16[128,256]{1,0:T(8,128)(2,1)S(1)}, u32[]{:S(2)}, u32[]{:S(2)}) collective-permute-start(bf16[128,256]{1,0:T(8,128)(2,1)} %refs_0_.1), channel_id=1, source_target_pairs={{0,6},{1,7},{2,4},{3,5},{4,2},{5,3},{6,0},{7,1},{8,14},{9,15},{10,... | collective-permute-start | bytes 196616 | tf_op jit(solution)/shard_map/ppermute | solution.py:313
  22.9 5.8 %collective-permute-start.6 = (bf16[128,256]{1,0:T(8,128)(2,1)}, bf16[128,256]{1,0:T(8,128)(2,1)S(1)}, u32[]{:S(2)}, u32[]{:S(2)}) collective-permute-start(bf16[128,256]{1,0:T(8,128)(2,1)} %refs_0_.1), channel_id=1, source_target_pairs={{0,7},{1,6},{2,5},{3,4},{4,3},{5,2},{6,1},{7,0},{8,15},{9,14},{10,... | collective-permute-start | bytes 196616 | tf_op jit(solution)/shard_map/ppermute | solution.py:313
  40.4 21.0 %all-to-all-start.1 = ((f32[32,24,128]{2,1,0:T(8,128)}), f32[32,24,128]{2,1,0:T(8,128)S(1)}, u32[]{:S(2)}, u32[]{:S(2)}) async-start(f32[32,24,128]{2,1,0:T(8,128)} %get-tuple-element.27), calls=%async_computation.1 | async-start | bytes 786432 | tf_op jit(solution)/shard_map/all_to_all | solution.py:25
  61.4 28.0 %copy-start = (f32[256]{0:T(256)S(1)}, f32[256]{0:T(256)}, u32[]{:S(2)}) copy-start(f32[256]{0:T(256)} %param.27) | copy-start | bytes 3076
  66.1 23.3 %all-to-all-start.2 = ((bf16[32,24,384]{2,1,0:T(8,128)(2,1)}), bf16[32,24,384]{2,1,0:T(8,128)(2,1)S(1)}, u32[]{:S(2)}, u32[]{:S(2)}) async-start(bf16[32,24,384]{2,1,0:T(8,128)(2,1)} %prompt_projection_out.1), calls=%async_computation.2 | async-start | bytes 1179648 | tf_op jit(solution)/shard_map/all_to_all | solution.py:25
  73.8 2.1 %collective-permute-start.7 = (f32[32,128]{1,0:T(8,128)S(1)}, f32[32,128]{1,0:T(8,128)S(1)}, u32[]{:S(2)}, u32[]{:S(2)}) collective-permute-start(f32[32,128]{1,0:T(8,128)S(1)} %get-tuple-element.17.lse), channel_id=1, source_target_pairs={{0,1},{1,0},{2,3},{3,2},{4,5},{5,4},{6,7},{7,6},{8,9},{9,8},{10,11... | collective-permute-start | bytes 49160 | tf_op jit(solution)/shard_map/ppermute | solution.py:397
  76.0 4.4 %collective-permute-start.8 = (f32[32,128]{1,0:T(8,128)S(1)}, f32[32,128]{1,0:T(8,128)S(1)}, u32[]{:S(2)}, u32[]{:S(2)}) collective-permute-start(f32[32,128]{1,0:T(8,128)S(1)} %multiply_add_fusion.2), channel_id=1, source_target_pairs={{0,2},{1,3},{2,0},{3,1},{4,6},{5,7},{6,4},{7,5},{8,10},{9,11},{10,... | collective-permute-start | bytes 49160 | tf_op jit(solution)/shard_map/ppermute | solution.py:397
  80.4 3.0 %collective-permute-start.9 = (f32[32,128]{1,0:T(8,128)S(1)}, f32[32,128]{1,0:T(8,128)S(1)}, u32[]{:S(2)}, u32[]{:S(2)}) collective-permute-start(f32[32,128]{1,0:T(8,128)S(1)} %multiply_add_fusion.1), channel_id=1, source_target_pairs={{0,4},{1,5},{2,6},{3,7},{4,0},{5,1},{6,2},{7,3},{8,12},{9,13},{10,... | collective-permute-start | bytes 49160 | tf_op jit(solution)/shard_map/ppermute | solution.py:397
  90.5 25.8 %copy-start.1 = (bf16[128,256]{1,0:T(8,128)(2,1)S(1)}, bf16[128,256]{1,0:T(8,128)(2,1)}, u32[]{:S(2)}) copy-start(bf16[128,256]{1,0:T(8,128)(2,1)} %refs_0_.1) | copy-start | bytes 196612
  90.5 25.8 %copy-start.3 = (f32[256]{0:T(256)S(1)}, f32[256]{0:T(256)}, u32[]{:S(2)}) copy-start(f32[256]{0:T(256)} %param.26) | copy-start | bytes 3076
  90.5 19.9 %all-to-all-start.3 = ((f32[8,24,256]{2,1,0:T(8,128)}), f32[8,24,256]{2,1,0:T(8,128)S(1)}, u32[]{:S(2)}, u32[]{:S(2)}) async-start(f32[8,24,256]{2,1,0:T(8,128)} %category_partial.1), calls=%async_computation.3 | async-start | bytes 393216 | tf_op jit(solution)/shard_map/all_to_all | solution.py:25
  97.7 19.4 %copy-start.2 = (bf16[24,256]{1,0:T(8,128)(2,1)S(1)}, bf16[24,256]{1,0:T(8,128)(2,1)}, u32[]{:S(2)}) copy-start(bf16[24,256]{1,0:T(8,128)(2,1)} %tokens.1) | copy-start | bytes 36868
  101.4 5.4 %collective-permute-start.10 = (bf16[128,256]{1,0:T(8,128)(2,1)S(1)}, bf16[128,256]{1,0:T(8,128)(2,1)S(1)}, u32[]{:S(2)}, u32[]{:S(2)}) collective-permute-start(bf16[128,256]{1,0:T(8,128)(2,1)S(1)} %get-tuple-element.20), channel_id=1, source_target_pairs={{0,1},{1,0},{2,3},{3,2},{4,5},{5,4},{6,7},{7,6},{8,9},{9,8},{10,11... | collective-permute-start | bytes 196616 | tf_op jit(solution)/shard_map/ppermute | solution.py:471
  101.6 7.9 %collective-permute-start.11 = (bf16[128,256]{1,0:T(8,128)(2,1)S(1)}, bf16[128,256]{1,0:T(8,128)(2,1)S(1)}, u32[]{:S(2)}, u32[]{:S(2)}) collective-permute-start(bf16[128,256]{1,0:T(8,128)(2,1)S(1)} %get-tuple-element.21), channel_id=1, source_target_pairs={{0,2},{1,3},{2,0},{3,1},{4,6},{5,7},{6,4},{7,5},{8,10},{9,11},{10,... | collective-permute-start | bytes 196616 | tf_op jit(solution)/shard_map/ppermute | solution.py:471
  104.7 11.5 %collective-permute-start.12 = (bf16[128,256]{1,0:T(8,128)(2,1)S(1)}, bf16[128,256]{1,0:T(8,128)(2,1)S(1)}, u32[]{:S(2)}, u32[]{:S(2)}) collective-permute-start(bf16[128,256]{1,0:T(8,128)(2,1)S(1)} %get-tuple-element.22), channel_id=1, source_target_pairs={{0,3},{1,2},{2,1},{3,0},{4,7},{5,6},{6,5},{7,4},{8,11},{9,10},{10,... | collective-permute-start | bytes 196616 | tf_op jit(solution)/shard_map/ppermute | solution.py:471
  105.1 11.1 %collective-permute-start.13 = (bf16[128,256]{1,0:T(8,128)(2,1)S(1)}, bf16[128,256]{1,0:T(8,128)(2,1)S(1)}, u32[]{:S(2)}, u32[]{:S(2)}) collective-permute-start(bf16[128,256]{1,0:T(8,128)(2,1)S(1)} %get-tuple-element.23), channel_id=1, source_target_pairs={{0,4},{1,5},{2,6},{3,7},{4,0},{5,1},{6,2},{7,3},{8,12},{9,13},{10,... | collective-permute-start | bytes 196616 | tf_op jit(solution)/shard_map/ppermute | solution.py:471
  106.5 9.8 %collective-permute-start.14 = (bf16[128,256]{1,0:T(8,128)(2,1)S(1)}, bf16[128,256]{1,0:T(8,128)(2,1)S(1)}, u32[]{:S(2)}, u32[]{:S(2)}) collective-permute-start(bf16[128,256]{1,0:T(8,128)(2,1)S(1)} %get-tuple-element.24), channel_id=1, source_target_pairs={{0,5},{1,4},{2,7},{3,6},{4,1},{5,0},{6,3},{7,2},{8,13},{9,12},{10,... | collective-permute-start | bytes 196616 | tf_op jit(solution)/shard_map/ppermute | solution.py:471
  106.8 9.5 %collective-permute-start.15 = (bf16[128,256]{1,0:T(8,128)(2,1)S(1)}, bf16[128,256]{1,0:T(8,128)(2,1)S(1)}, u32[]{:S(2)}, u32[]{:S(2)}) collective-permute-start(bf16[128,256]{1,0:T(8,128)(2,1)S(1)} %get-tuple-element.25), channel_id=1, source_target_pairs={{0,6},{1,7},{2,4},{3,5},{4,2},{5,3},{6,0},{7,1},{8,14},{9,15},{10,... | collective-permute-start | bytes 196616 | tf_op jit(solution)/shard_map/ppermute | solution.py:471
  109.5 6.8 %collective-permute-start.16 = (bf16[128,256]{1,0:T(8,128)(2,1)S(1)}, bf16[128,256]{1,0:T(8,128)(2,1)S(1)}, u32[]{:S(2)}, u32[]{:S(2)}) collective-permute-start(bf16[128,256]{1,0:T(8,128)(2,1)S(1)} %get-tuple-element.26), channel_id=1, source_target_pairs={{0,7},{1,6},{2,5},{3,4},{4,3},{5,2},{6,1},{7,0},{8,15},{9,14},{10,... | collective-permute-start | bytes 196616 | tf_op jit(solution)/shard_map/ppermute | solution.py:471
  111.1 15.2 %all-to-all-start.4 = ((bf16[32,24,128]{2,1,0:T(8,128)(2,1)}), bf16[32,24,128]{2,1,0:T(8,128)(2,1)S(1)}, u32[]{:S(2)}, u32[]{:S(2)}) async-start(bf16[32,24,128]{2,1,0:T(8,128)(2,1)} %category_mean.1), calls=%async_computation.4 | async-start | bytes 393216 | tf_op jit(solution)/shard_map/all_to_all | solution.py:25

commit v3 on v2

--- a/solution.py
+++ b/solution.py
@@ -1,3 +1,4 @@
+import functools
 import math
 
 import jax
@@ -11,12 +12,15 @@
 
 HD = 256
 CHUNK = 256
+PAIRED = 2
 EPSILON = 1e-05
 MASKED = -1e30
 ALL = ("x", "z", "yl", "yh", "c")
 PROMPT_ORDER = ("yh", "c", "x", "z", "yl")
 PLANE = ("x", "z")
 COLUMN = ("yl", "yh", "c")
+LINE = ("yl", "yh")
+CORE = "c"
 BF = jnp.bfloat16
 F32 = jnp.float32
 
@@ -88,8 +92,13 @@
 
 
 def attend(reduced, kept, values_t, bias, out_t, lse, head):
-    for at in range(0, kept.shape[0], CHUNK):
-        scores = dot_nt(reduced, kept[at : at + CHUNK])
+    rows = kept.shape[0] // 128
+    starts = range(0, kept.shape[0], CHUNK)
+    following = dot_nt(reduced, kept[:CHUNK])
+    for at in starts:
+        scores = following
+        if at + CHUNK < kept.shape[0]:
+            following = dot_nt(reduced, kept[at + CHUNK : at + 2 * CHUNK])
         if bias is not None:
             scores = scores + bias
         top = jnp.max(scores, axis=0, keepdims=True)
@@ -98,7 +107,6 @@
         numer = dot(values_t, weights.astype(BF))
         out_t[:, at : at + CHUNK] = (numer * (1.0 / total)).astype(BF)
         stat = top + jnp.log2(total)
-        rows = kept.shape[0] // 128
         for k in range(CHUNK // 128):
             lse[pl.ds(head * rows + at // 128 + k, 1), :] = stat[:, k * 128 : (k + 1) * 128]
 
@@ -114,13 +122,20 @@
     return (dot(images[...], query_w[...]) * factor).astype(BF)
 
 
+def join_halves(core, own, other, held):
+    rows = own.shape[0]
+    held[pl.ds(pl.multiple_of(core[0] * rows, rows), rows), :] = own[...]
+    held[pl.ds(pl.multiple_of((1 - core[0]) * rows, rows), rows), :] = other[...]
+
+
 def column_kernel(
-    images, packed, gain, query_w, value_w, key_w, out_t, lse, lse_copies, held
+    core, own, other, packed, gain, query_w, value_w, key_w, out_t, lse, lse_copies, images, held
 ):
     head = pl.program_id(0)
 
     @pl.when(head == 0)
     def _():
+        join_halves(core, own, other, images)
         held[...] = normed(tokens_of(packed), gain[...])
 
     values_t = dot_nt(value_w[...].T, images[...]).astype(BF)
@@ -130,12 +145,13 @@
 
 
 def row_kernel(
-    images, packed, gain, query_w, key_w, value_w, out_t, lse, members, held, bias
+    core, own, other, packed, gain, query_w, key_w, value_w, out_t, lse, members, images, held, bias
 ):
     head = pl.program_id(0)
 
     @pl.when(head == 0)
     def _():
+        join_halves(core, own, other, images)
         held[...] = normed(tokens_of(packed), gain[...])
         codes = codes_of(packed)
         members[...] = members_of(codes, 0, members.shape[0]).astype(BF)
@@ -147,26 +163,31 @@
 
 
 def add_projected(share, out_t, out_w, total):
+    step = pl.program_id(0)
+    group = out_t.shape[0] // HD
+    rows = share.shape[0] // (pl.num_programs(0) * group)
+    term = None
+    for k in range(group):
+        at = (step * group + k) * rows
+        line = jnp.concatenate([share[pl.ds(at + r, 1), :] for r in range(rows)], axis=1)
+        block = slice(k * HD, (k + 1) * HD)
+        part = dot(out_w[block, :].T, (out_t[block, :] * line).astype(BF))
+        term = part if term is None else term + part
+
+    @pl.when(step == 0)
+    def _():
+        total[...] = term
+
+    @pl.when(step > 0)
+    def _():
+        total[...] += term
+
+
+def image_out_kernel(core, lse_whole, lse, out_t, out_w, own, other, share, total, turned):
     head = pl.program_id(0)
-    rows = share.shape[0] // pl.num_programs(0)
-    line = jnp.concatenate([share[pl.ds(head * rows + k, 1), :] for k in range(rows)], axis=1)
-    term = dot(out_w[...].T, (out_t[...] * line).astype(BF))
 
     @pl.when(head == 0)
     def _():
-        total[...] = term
-
-    @pl.when(head > 0)
-    def _():
-        total[...] += term
-
-
-def image_out_kernel(place, lse_whole, lse, out_t, out_w, *refs):
-    *sent, share, total, turned = refs
-    head = pl.program_id(0)
-
-    @pl.when(head == 0)
-    def _():
         share[...] = jnp.exp2(lse[...] - lse_whole[...])
 
     add_projected(share, out_t, out_w, total)
@@ -174,9 +195,16 @@
     @pl.when(head == pl.num_programs(0) - 1)
     def _():
         turned[...] = total[...].T.astype(BF)
-        for k, part in enumerate(sent):
-            rows = part.shape[0]
-            part[...] = turned[pl.ds(pl.multiple_of((place[0] ^ k) * rows, rows), rows), :]
+        rows = own.shape[0]
+        own[...] = turned[pl.ds(pl.multiple_of(core[0] * rows, rows), rows), :]
+        other[...] = turned[pl.ds(pl.multiple_of((1 - core[0]) * rows, rows), rows), :]
+
+
+def image_sum_kernel(place, own, arrived, *sent):
+    for k, part in enumerate(sent):
+        rows = part.shape[0]
+        at = pl.ds(pl.multiple_of((place[0] ^ k) * rows, rows), rows)
+        part[...] = (own[at, :].astype(F32) + arrived[at, :].astype(F32)).astype(BF)
 
 
 def members_of(codes, first, count):
@@ -307,35 +335,42 @@
         name="pack",
     )(*kept_far(prompt_tokens, category_ids.reshape(1, -1), prompt_valid.reshape(1, -1)))
     prompt_all = swap(packed, PLANE)
+    line = lax.axis_size(LINE)
+    half = images // 2
+    swapped = [(0, 1), (1, 0)]
     image_parts = [image_tokens]
-    for k in range(1, columns):
-        turned = [(i, i ^ k) for i in range(columns)]
-        image_parts.append(lax.ppermute(image_tokens, COLUMN, turned))
+    for k in range(1, line):
+        image_parts.append(lax.ppermute(image_tokens, LINE, [(i, i ^ k) for i in range(line)]))
 
     head_columns = lambda n: block((n, HD), lambda h: (0, h))
     head_rows = lambda n: block((HD, n), lambda h: (h, 0))
+    pair_rows = lambda n: block((PAIRED * HD, n), lambda h: (h, 0))
     row = lambda n: block((1, n), lambda h: (0, 0))
 
     pair_flops = 4 * images * prompts * width
     stat_rows = heads * prompts // 128
     stats = lambda n: block((n, 128), lambda h: (0, 0))
     scalar = pl.BlockSpec(memory_space=pltpu.SMEM)
-    column_place = lax.axis_index(COLUMN).astype(jnp.int32).reshape(1)
+    line_place = lax.axis_index(LINE).astype(jnp.int32).reshape(1)
+    core = lax.axis_index(CORE).astype(jnp.int32).reshape(1)
     image_row = image_gain.reshape(1, depth)
     prompt_row = prompt_gain.reshape(1, depth)
-    image_normed = pl.pallas_call(
+    image_own = pl.pallas_call(
         image_norm_kernel,
-        in_specs=[scalar] + [pl.BlockSpec(memory_space=pltpu.VMEM)] * (columns + 1),
-        out_shape=shaped((images, depth), BF),
+        in_specs=[scalar] + [pl.BlockSpec(memory_space=pltpu.VMEM)] * (line + 1),
+        out_shape=shaped((half, depth), BF),
         compiler_params=params(),
-        cost_estimate=cost(10 * images * depth, 4 * images * depth),
+        cost_estimate=cost(10 * half * depth, 4 * half * depth),
         name="image_norm",
-    )(column_place, *kept_far(image_tokens), *image_parts[1:], *kept_far(image_row))
+    )(line_place, *kept_far(image_tokens), *image_parts[1:], *kept_far(image_row))
+    image_other = lax.ppermute(image_own, CORE, swapped)
     prompt_part_t, col_lse, col_lse_copies = pl.pallas_call(
         column_kernel,
         grid=(heads,),
         in_specs=[
-            whole(image_normed),
+            scalar,
+            whole(image_own),
+            whole(image_other),
             whole(prompt_all),
             row(depth),
             head_columns(depth),
@@ -352,11 +387,17 @@
             shaped((stat_rows, 128), F32),
             shaped((planes, stat_rows, 128), F32),
         ],
-        scratch_shapes=[pltpu.VMEM((prompts, depth), BF)],
+        scratch_shapes=[pltpu.VMEM((images, depth), BF), pltpu.VMEM((prompts, depth), BF)],
         compiler_params=params(dimension_semantics=("arbitrary",)),
         cost_estimate=cost(2 * pair_flops, 6 * images * width, images * prompts * heads),
         name="column_attention",
-    )(image_normed, prompt_all, *kept_far(prompt_row, query_weight, image_value_weight, key_weight))
+    )(
+        core,
+        image_own,
+        image_other,
+        prompt_all,
+        *kept_far(prompt_row, query_weight, image_value_weight, key_weight),
+    )
 
     col_lse_all = swap(col_lse_copies, PLANE)
 
@@ -365,7 +406,9 @@
         row_kernel,
         grid=(heads,),
         in_specs=[
-            whole(image_normed),
+            scalar,
+            whole(image_own),
+            whole(image_other),
             whole(prompt_all),
             row(depth),
             head_columns(depth),
@@ -382,31 +425,41 @@
             shaped((row_stat_rows, 128), F32),
             far((categories, prompts), BF),
         ],
-        scratch_shapes=[pltpu.VMEM((prompts, depth), BF), pltpu.VMEM((prompts, 128), F32)],
+        scratch_shapes=[
+            pltpu.VMEM((images, depth), BF),
+            pltpu.VMEM((prompts, depth), BF),
+            pltpu.VMEM((prompts, 128), F32),
+        ],
         compiler_params=params(dimension_semantics=("arbitrary",)),
         cost_estimate=cost(2 * pair_flops, 6 * images * width, images * prompts * heads),
         name="row_attention",
     )(
-        image_normed,
+        core,
+        image_own,
+        image_other,
         prompt_all,
         *kept_far(prompt_row, query_weight, key_weight, prompt_value_weight),
     )
 
-    row_whole = row_lse
-    for bit in (1, 2, 4):
-        other = lax.ppermute(row_whole, COLUMN, [(i, i ^ bit) for i in range(columns)])
-        apart = jnp.exp2(-jnp.abs(row_whole - other))
-        row_whole = jnp.maximum(row_whole, other) + jnp.log2(1.0 + apart)
+    def mixed(parts):
+        top = functools.reduce(jnp.maximum, parts)
+        return top + jnp.log2(sum(jnp.exp2(part - top) for part in parts))
+
+    row_parts = [row_lse]
+    for k in range(1, line):
+        row_parts.append(lax.ppermute(row_lse, LINE, [(i, i ^ k) for i in range(line)]))
+    row_own = mixed(row_parts)
+    row_whole = mixed([row_own, lax.ppermute(row_own, CORE, swapped)])
 
     plane_sent = pl.pallas_call(
         prompt_out_kernel,
-        grid=(heads,),
+        grid=(heads // PAIRED,),
         in_specs=[
             whole(col_lse_all),
             whole(col_lse),
-            head_rows(prompts),
-            head_rows(depth),
-            block((categories // heads, prompts), lambda h: (h, 0)),
+            pair_rows(prompts),
+            pair_rows(depth),
+            block((categories * PAIRED // heads, prompts), lambda h: (h, 0)),
         ],
         out_specs=block((planes, own_prompts, depth + 128), lambda h: (0, 0, 0)),
         out_shape=shaped((planes, own_prompts, depth + 128), BF),
@@ -421,12 +474,12 @@
     )(col_lse_all, col_lse, *kept_far(prompt_part_t, prompt_out_weight, members))
     plane_arrived = swap(plane_sent, PLANE)
 
-    image_sent = pl.pallas_call(
+    own_sum, other_sum = pl.pallas_call(
         image_out_kernel,
-        grid=(heads,),
-        in_specs=[scalar, whole(row_whole), whole(row_lse), head_rows(images), head_rows(depth)],
-        out_specs=[block((own_images, depth), lambda h: (0, 0))] * columns,
-        out_shape=[shaped((own_images, depth), BF)] * columns,
+        grid=(heads // PAIRED,),
+        in_specs=[scalar, whole(row_whole), whole(row_lse), pair_rows(images), pair_rows(depth)],
+        out_specs=[block((half, depth), lambda h: (0, 0))] * 2,
+        out_shape=[shaped((half, depth), BF)] * 2,
         scratch_shapes=[
             pltpu.VMEM(row_lse.shape, F32),
             pltpu.VMEM((depth, images), F32),
@@ -435,7 +488,7 @@
         compiler_params=params(dimension_semantics=("arbitrary",)),
         cost_estimate=cost(2 * images * depth * width, 6 * images * width),
         name="image_projection_out",
-    )(column_place, row_whole, row_lse, *kept_far(image_part_t, image_out_weight))
+    )(core, row_whole, row_lse, *kept_far(image_part_t, image_out_weight))
 
     category_copies = pl.pallas_call(
         category_kernel,
@@ -465,10 +518,19 @@
         name="category_table",
     )(mean_all)
 
+    crossed_sum = lax.ppermute(other_sum, CORE, swapped)
+    image_sent = pl.pallas_call(
+        image_sum_kernel,
+        in_specs=[scalar] + [pl.BlockSpec(memory_space=pltpu.VMEM)] * 2,
+        out_shape=[shaped((own_images, depth), BF)] * line,
+        compiler_params=params(),
+        cost_estimate=cost(half * depth, 6 * half * depth),
+        name="image_sum",
+    )(line_place, own_sum, crossed_sum)
     image_delta = image_sent[0].astype(F32)
-    for k in range(1, columns):
-        turned = [(i, i ^ k) for i in range(columns)]
-        image_delta += lax.ppermute(image_sent[k], COLUMN, turned).astype(F32)
+    for k in range(1, line):
+        turned = [(i, i ^ k) for i in range(line)]
+        image_delta += lax.ppermute(image_sent[k], LINE, turned).astype(F32)
     joined_image = (image_tokens.astype(F32) + image_layer_scale * image_delta).astype(BF)
     prompt_delta = jnp.sum(plane_arrived[:, :, :depth].astype(F32), axis=0)
     joined_prompt = (prompt_tokens.astype(F32) + prompt_layer_scale * prompt_delta).astype(BF)

time: 128 us -> 117 us (0.914)
  waiting for transfers between devices: 28.2 us -> 21.9 us
  Pallas kernels: 34.5 us -> 31.4 us
  starting transfers between devices: 62.2 us -> 59.6 us
    ppermute x17 -> x12, waiting for transfers between devices: 11.9 us -> 7.76 us  [the longest x3 4.45 us: on_device(): lax.ppermute(image_tokens, LINE, [(i, i ^ k) for i in range(line)])]
    ppermute x17 -> x12, starting transfers between devices: 21.1 us -> 18.2 us  [the longest x3 3.97 us: on_device(): image_delta += lax.ppermute(image_sent[k], LINE, turned).astype(F32)]
    pallas_call x4 -> x5, Pallas kernels: 29 us -> 26.2 us  [the longest x1 10.3 us: on_device(): pl.pallas_call(row_kernel, grid=(heads,), in_specs=[scalar, whole(image_o...]
    all_to_all x5, waiting for transfers between devices: 16.2 us -> 14.2 us  [swap(): return lax.all_to_all(parts, axes, split_axis=0, concat_axis=0, tiled=True)]
  transfers between devices with their start and end apart: 22 -> 17, of which waited for: 9 -> 11; matrix products, arithmetic and copies ran while one was open for 1% -> 1% of each run, Pallas kernels for 13% -> 14%
where the time goes in v3:
time: 117 us; the launch traced here: 115 us
  starting transfers between devices  59.6 us (51%)
  Pallas kernels  31.4 us (27%)
  waiting for transfers between devices  21.9 us (19%)
  other arithmetic  1.42 us (1%)
    all_to_all x5, starting transfers between devices, swap(): return lax.all_to_all(parts, axes, split_axis=0, concat_axis=0, tiled=True)  41.3 us
    all_to_all x5, waiting for transfers between devices, swap(): return lax.all_to_all(parts, axes, split_axis=0, concat_axis=0, tiled=True)  14.2 us
    pallas_call x1, Pallas kernels, on_device(): pl.pallas_call(row_kernel, grid=(heads,), in_specs=[scalar, whole(image_o...  10.3 us
    pallas_call x1, Pallas kernels, on_device(): pl.pallas_call(column_kernel, grid=(heads,), in_specs=[scalar, whole(imag...  9.62 us
    ppermute x3, waiting for transfers between devices, on_device(): lax.ppermute(image_tokens, LINE, [(i, i ^ k) for i in range(line)])  4.45 us
    ppermute x3, starting transfers between devices, on_device(): image_delta += lax.ppermute(image_sent[k], LINE, turned).astype(F32)  3.97 us
    ppermute x3, starting transfers between devices, on_device(): lax.ppermute(row_lse, LINE, [(i, i ^ k) for i in range(line)])  3.95 us
    ppermute x3, starting transfers between devices, on_device(): lax.ppermute(image_tokens, LINE, [(i, i ^ k) for i in range(line)])  3.78 us
  transfers between devices with their start and end apart: 17, of which 11 were waited for; matrix products, arithmetic and copies ran while one was open for 1% of the time, Pallas kernels for 14%

profile of v3, /device:TPU:1, one launch (start us, length us, event | category | flops | bytes accessed | tf_op | source)
XLA Modules:
  0.0 115.1 jit_solution(13656170929103169467)
XLA Ops:
  0.6 1.6 %pack.1 = bf16[32,56,128]{2,1,0:T(8,128)(2,1)} custom-call(bf16[24,256]{1,0:T(8,128)(2,1)} %tokens.1, s32[1,24]{1,0:T(1,128)} %bitcast.10, s32[1,24]{1,0:T(1,128)} %bitcast.11), custom_call_target="tpu_custom_call" | custom-call | tf_op jit(solution)/shard_map/pack/pallas_call | solution.py:331
  2.2 11.9 %all-to-all-start = ((bf16[32,56,128]{2,1,0:T(8,128)(2,1)}), bf16[32,56,128]{2,1,0:T(8,128)(2,1)S(1)}, u32[]{:S(2)}, u32[]{:S(2)}) async-start(bf16[32,56,128]{2,1,0:T(8,128)(2,1)} %pack.1), calls=%async_computation | async-start | bytes 917504 | tf_op jit(solution)/shard_map/all_to_all | solution.py:29
  14.1 3.0 %collective-permute-start = (bf16[128,256]{1,0:T(8,128)(2,1)}, bf16[128,256]{1,0:T(8,128)(2,1)S(1)}, u32[]{:S(2)}, u32[]{:S(2)}) collective-permute-start(bf16[128,256]{1,0:T(8,128)(2,1)} %refs_0_.1), channel_id=1, source_target_pairs={{0,2},{2,0},{4,6},{6,4},{1,3},{3,1},{5,7},{7,5},{8,10},{10,8},{12,... | collective-permute-start | bytes 196616 | tf_op jit(solution)/shard_map/ppermute | solution.py:343
  17.1 0.4 collective-permute-start.1
  17.5 0.4 collective-permute-start.2
  17.9 1.1 collective-permute-done.refs_1_
  19.0 1.9 %collective-permute-done.1.refs_2_ = bf16[128,256]{1,0:T(8,128)(2,1)S(1)} collective-permute-done((bf16[128,256]{1,0:T(8,128)(2,1)}, bf16[128,256]{1,0:T(8,128)(2,1)S(1)}, u32[]{:S(2)}, u32[]{:S(2)}) %collective-permute-start.1) | collective-permute-done | bytes 65568 | tf_op jit(solution)/shard_map/ppermute | solution.py:343
  20.9 1.4 %collective-permute-done.2.refs_3_ = bf16[128,256]{1,0:T(8,128)(2,1)S(1)} collective-permute-done((bf16[128,256]{1,0:T(8,128)(2,1)}, bf16[128,256]{1,0:T(8,128)(2,1)S(1)}, u32[]{:S(2)}, u32[]{:S(2)}) %collective-permute-start.2) | collective-permute-done | bytes 65568 | tf_op jit(solution)/shard_map/ppermute | solution.py:343
  22.3 1.1 image_norm.1.own
  23.4 2.5 %collective-permute-start.3 = (bf16[512,256]{1,0:T(8,128)(2,1)S(1)}, bf16[512,256]{1,0:T(8,128)(2,1)S(1)}, u32[]{:S(2)}, u32[]{:S(2)}) collective-permute-start(bf16[512,256]{1,0:T(8,128)(2,1)S(1)} %image_norm.1.own), channel_id=1, source_target_pairs={{0,1},{1,0},{2,3},{3,2},{4,5},{5,4},{6,7},{7,6},{8,9},{9,8},{10,11... | collective-permute-start | bytes 786440 | tf_op jit(solution)/shard_map/ppermute | solution.py:366
  25.9 1.2 %collective-permute-done.3.other = bf16[512,256]{1,0:T(8,128)(2,1)S(1)} collective-permute-done((bf16[512,256]{1,0:T(8,128)(2,1)S(1)}, bf16[512,256]{1,0:T(8,128)(2,1)S(1)}, u32[]{:S(2)}, u32[]{:S(2)}) %collective-permute-start.3) | collective-permute-done | bytes 262176 | tf_op jit(solution)/shard_map/ppermute | solution.py:366
  27.0 0.1 all-to-all-done.packed
  27.1 9.6 %column_attention.1 = (bf16[1024,768]{1,0:T(8,128)(2,1)}, f32[24,128]{1,0:T(8,128)S(1)}, f32[32,24,128]{2,1,0:T(8,128)}) custom-call(s32[1]{0:T(128)} %bitcast.1.core, bf16[512,256]{1,0:T(8,128)(2,1)S(1)} %image_norm.1.own, bf16[512,256]{1,0:T(8,128)(2,1)S(1)} %collective-permute-done.3.other, bf16[32,56,128]{2,1,0:T(8,128)(2,1)S(1)} %all-to-all-done.packed, ...), custom_call_target="tpu_custom_call" | custom-call | flops 6442450944 | bytes 6291456 | tf_op jit(solution)/shard_map/column_attention/pallas_call | solution.py:367
  36.7 9.4 %all-to-all-start.1 = ((f32[32,24,128]{2,1,0:T(8,128)}), f32[32,24,128]{2,1,0:T(8,128)S(1)}, u32[]{:S(2)}, u32[]{:S(2)}) async-start(f32[32,24,128]{2,1,0:T(8,128)} %get-tuple-element.23), calls=%async_computation.1 | async-start | bytes 786432 | tf_op jit(solution)/shard_map/all_to_all | solution.py:29
  46.2 10.3 %row_attention.1 = (bf16[1024,1024]{1,0:T(8,128)(2,1)}, f32[32,128]{1,0:T(8,128)S(1)}, bf16[384,768]{1,0:T(8,128)(2,1)}) custom-call(s32[1]{0:T(128)} %bitcast.1.core, bf16[512,256]{1,0:T(8,128)(2,1)S(1)} %image_norm.1.own, bf16[512,256]{1,0:T(8,128)(2,1)S(1)} %collective-permute-done.3.other, bf16[32,56,128]{2,1,0:T(8,128)(2,1)S(1)} %all-to-all-done.packed, ...), custom_call_target="tpu_custom_call" | custom-call | flops 6442450944 | bytes 6291456 | tf_op jit(solution)/shard_map/row_attention/pallas_call | solution.py:405
  56.4 1.5 %all-to-all-done.1.lse_all = f32[32,24,128]{2,1,0:T(8,128)S(1)} async-done(((f32[32,24,128]{2,1,0:T(8,128)}), f32[32,24,128]{2,1,0:T(8,128)S(1)}, u32[]{:S(2)}, u32[]{:S(2)}) %all-to-all-start.1) | async-done | bytes 393248 | tf_op jit(solution)/shard_map/all_to_all | solution.py:29
  58.0 3.6 %prompt_projection_out.1 = bf16[32,24,384]{2,1,0:T(8,128)(2,1)} custom-call(f32[32,24,128]{2,1,0:T(8,128)S(1)} %all-to-all-done.1.lse_all, f32[24,128]{1,0:T(8,128)S(1)} %get-tuple-element.24.lse, bf16[1024,768]{1,0:T(8,128)(2,1)} %get-tuple-element.25.out_t, bf16[1024,256]{1,0:T(8,128)(2,1)} %out_w.3, bf16[384,768]{1,0:T(8,128)(2,1)} %get-tuple-element.26.members), custom_call_target="tpu_custom_call" | custom-call | flops 553648128 | bytes 4718592 | tf_op jit(solution)/shard_map/prompt_projection_out/pallas_call | solution.py:454
  61.6 0.0 copy-start
  61.6 7.8 %all-to-all-start.2 = ((bf16[32,24,384]{2,1,0:T(8,128)(2,1)}), bf16[32,24,384]{2,1,0:T(8,128)(2,1)S(1)}, u32[]{:S(2)}, u32[]{:S(2)}) async-start(bf16[32,24,384]{2,1,0:T(8,128)(2,1)} %prompt_projection_out.1), calls=%async_computation.2 | async-start | bytes 1179648 | tf_op jit(solution)/shard_map/all_to_all | solution.py:29
  69.4 1.1 collective-permute-start.6
  70.5 0.0 collective-permute-start.5
  70.5 2.9 %collective-permute-start.4 = (f32[32,128]{1,0:T(8,128)S(1)}, f32[32,128]{1,0:T(8,128)S(1)}, u32[]{:S(2)}, u32[]{:S(2)}) collective-permute-start(f32[32,128]{1,0:T(8,128)S(1)} %get-tuple-element.15.lse), channel_id=1, source_target_pairs={{0,2},{2,0},{4,6},{6,4},{1,3},{3,1},{5,7},{7,5},{8,10},{10,8},{12,... | collective-permute-start | bytes 49160 | tf_op jit(solution)/shard_map/ppermute | solution.py:450
  73.4 0.0 collective-permute-done.6
  73.4 0.0 collective-permute-done.5
  73.4 1.3 %collective-permute-done.4 = f32[32,128]{1,0:T(8,128)S(1)} collective-permute-done((f32[32,128]{1,0:T(8,128)S(1)}, f32[32,128]{1,0:T(8,128)S(1)}, u32[]{:S(2)}, u32[]{:S(2)}) %collective-permute-start.4) | collective-permute-done | bytes 16416 | tf_op jit(solution)/shard_map/ppermute | solution.py:450
  74.7 3.6 %collective-permute-start.7 = (f32[32,128]{1,0:T(8,128)S(1)}, f32[32,128]{1,0:T(8,128)S(1)}, u32[]{:S(2)}, u32[]{:S(2)}) collective-permute-start(f32[32,128]{1,0:T(8,128)S(1)} %multiply_add_fusion.1), channel_id=1, source_target_pairs={{0,1},{1,0},{2,3},{3,2},{4,5},{5,4},{6,7},{7,6},{8,9},{9,8},{10,11... | collective-permute-start | bytes 49160 | tf_op jit(solution)/shard_map/ppermute | solution.py:452
  78.3 0.8 collective-permute-done.7
  79.2 2.7 %image_projection_out.1 = (bf16[512,256]{1,0:T(8,128)(2,1)S(1)}, bf16[512,256]{1,0:T(8,128)(2,1)S(1)}) custom-call(s32[1]{0:T(128)} %bitcast.1.core, f32[32,128]{1,0:T(8,128)S(1)} %multiply_add_fusion.lse_whole, f32[32,128]{1,0:T(8,128)S(1)} %get-tuple-element.15.lse, bf16[1024,1024]{1,0:T(8,128)(2,1)} %get-tuple-element.16.out_t, bf16[1024,256]{1,0:T(8,128)(2,1)} %out_w.2), custom_call_target="tpu_custom_call" | custom-call | flops 536870912 | bytes 6291456 | tf_op jit(solution)/shard_map/image_projection_out/pallas_call | solution.py:477
  81.9 0.0 copy-start.1
  81.9 0.0 copy-start.3
  81.9 0.0 copy-start.2
  81.9 0.4 collective-permute-start.8
  82.3 2.7 %all-to-all-done.2.arrived = bf16[32,24,384]{2,1,0:T(8,128)(2,1)S(1)} async-done(((bf16[32,24,384]{2,1,0:T(8,128)(2,1)}), bf16[32,24,384]{2,1,0:T(8,128)(2,1)S(1)}, u32[]{:S(2)}, u32[]{:S(2)}) %all-to-all-start.2) | async-done | bytes 589856 | tf_op jit(solution)/shard_map/all_to_all | solution.py:29
  85.1 0.0 copy-done
  85.1 1.0 category_partial.1
  86.0 7.1 %all-to-all-start.3 = ((f32[8,24,256]{2,1,0:T(8,128)}), f32[8,24,256]{2,1,0:T(8,128)S(1)}, u32[]{:S(2)}, u32[]{:S(2)}) async-start(f32[8,24,256]{2,1,0:T(8,128)} %category_partial.1), calls=%async_computation.3 | async-start | bytes 393216 | tf_op jit(solution)/shard_map/all_to_all | solution.py:29
  93.1 0.0 collective-permute-done.8.arrived
  93.1 0.1 image_sum.1
  93.2 2.7 %collective-permute-start.11 = (bf16[128,256]{1,0:T(8,128)(2,1)S(1)}, bf16[128,256]{1,0:T(8,128)(2,1)S(1)}, u32[]{:S(2)}, u32[]{:S(2)}) collective-permute-start(bf16[128,256]{1,0:T(8,128)(2,1)S(1)} %get-tuple-element.22), channel_id=1, source_target_pairs={{0,6},{2,4},{4,2},{6,0},{1,7},{3,5},{5,3},{7,1},{8,14},{10,12},{12... | collective-permute-start | bytes 196616 | tf_op jit(solution)/shard_map/ppermute | solution.py:533
  95.9 0.0 collective-permute-start.10
  95.9 1.3 %collective-permute-start.9 = (bf16[128,256]{1,0:T(8,128)(2,1)S(1)}, bf16[128,256]{1,0:T(8,128)(2,1)S(1)}, u32[]{:S(2)}, u32[]{:S(2)}) collective-permute-start(bf16[128,256]{1,0:T(8,128)(2,1)S(1)} %get-tuple-element.20), channel_id=1, source_target_pairs={{0,2},{2,0},{4,6},{6,4},{1,3},{3,1},{5,7},{7,5},{8,10},{10,8},{12,... | collective-permute-start | bytes 196616 | tf_op jit(solution)/shard_map/ppermute | solution.py:533
  97.1 1.9 %all-to-all-done.3.partials = f32[8,24,256]{2,1,0:T(8,128)S(1)} async-done(((f32[8,24,256]{2,1,0:T(8,128)}), f32[8,24,256]{2,1,0:T(8,128)S(1)}, u32[]{:S(2)}, u32[]{:S(2)}) %all-to-all-start.3) | async-done | bytes 196640 | tf_op jit(solution)/shard_map/all_to_all | solution.py:29
  99.0 0.7 category_mean.1
  99.7 5.2 %all-to-all-start.4 = ((bf16[32,24,128]{2,1,0:T(8,128)(2,1)}), bf16[32,24,128]{2,1,0:T(8,128)(2,1)S(1)}, u32[]{:S(2)}, u32[]{:S(2)}) async-start(bf16[32,24,128]{2,1,0:T(8,128)(2,1)} %category_mean.1), calls=%async_computation.4 | async-start | bytes 393216 | tf_op jit(solution)/shard_map/all_to_all | solution.py:29
  104.9 0.0 collective-permute-done.11
  104.9 0.0 collective-permute-done.10
  104.9 0.0 collective-permute-done.9
  104.9 0.0 copy-done.1
  105.0 0.0 copy-done.3
  105.0 0.7 add_convert_fusion
  105.6 0.1 convert_reduce_fusion
  105.7 0.0 copy-done.2
  105.7 0.6 add_convert_fusion.1
  106.3 8.0 %all-to-all-done.4.pieces = bf16[32,24,128]{2,1,0:T(8,128)(2,1)S(1)} async-done(((bf16[32,24,128]{2,1,0:T(8,128)(2,1)}), bf16[32,24,128]{2,1,0:T(8,128)(2,1)S(1)}, u32[]{:S(2)}, u32[]{:S(2)}) %all-to-all-start.4) | async-done | bytes 196640 | tf_op jit(solution)/shard_map/all_to_all | solution.py:29
  114.3 0.8 category_table.1
  (2 shorter events, 0.1 us)
Async XLA Ops:
  2.2 24.9 %all-to-all-start = ((bf16[32,56,128]{2,1,0:T(8,128)(2,1)}), bf16[32,56,128]{2,1,0:T(8,128)(2,1)S(1)}, u32[]{:S(2)}, u32[]{:S(2)}) async-start(bf16[32,56,128]{2,1,0:T(8,128)(2,1)} %pack.1), calls=%async_computation | async-start | bytes 917504 | tf_op jit(solution)/shard_map/all_to_all | solution.py:29
  14.1 4.9 %collective-permute-start = (bf16[128,256]{1,0:T(8,128)(2,1)}, bf16[128,256]{1,0:T(8,128)(2,1)S(1)}, u32[]{:S(2)}, u32[]{:S(2)}) collective-permute-start(bf16[128,256]{1,0:T(8,128)(2,1)} %refs_0_.1), channel_id=1, source_target_pairs={{0,2},{2,0},{4,6},{6,4},{1,3},{3,1},{5,7},{7,5},{8,10},{10,8},{12,... | collective-permute-start | bytes 196616 | tf_op jit(solution)/shard_map/ppermute | solution.py:343
  17.1 3.8 %collective-permute-start.1 = (bf16[128,256]{1,0:T(8,128)(2,1)}, bf16[128,256]{1,0:T(8,128)(2,1)S(1)}, u32[]{:S(2)}, u32[]{:S(2)}) collective-permute-start(bf16[128,256]{1,0:T(8,128)(2,1)} %refs_0_.1), channel_id=1, source_target_pairs={{0,4},{2,6},{4,0},{6,2},{1,5},{3,7},{5,1},{7,3},{8,12},{10,14},{12... | collective-permute-start | bytes 196616 | tf_op jit(solution)/shard_map/ppermute | solution.py:343
  17.5 4.8 %collective-permute-start.2 = (bf16[128,256]{1,0:T(8,128)(2,1)}, bf16[128,256]{1,0:T(8,128)(2,1)S(1)}, u32[]{:S(2)}, u32[]{:S(2)}) collective-permute-start(bf16[128,256]{1,0:T(8,128)(2,1)} %refs_0_.1), channel_id=1, source_target_pairs={{0,6},{2,4},{4,2},{6,0},{1,7},{3,5},{5,3},{7,1},{8,14},{10,12},{12... | collective-permute-start | bytes 196616 | tf_op jit(solution)/shard_map/ppermute | solution.py:343
  23.4 3.6 %collective-permute-start.3 = (bf16[512,256]{1,0:T(8,128)(2,1)S(1)}, bf16[512,256]{1,0:T(8,128)(2,1)S(1)}, u32[]{:S(2)}, u32[]{:S(2)}) collective-permute-start(bf16[512,256]{1,0:T(8,128)(2,1)S(1)} %image_norm.1.own), channel_id=1, source_target_pairs={{0,1},{1,0},{2,3},{3,2},{4,5},{5,4},{6,7},{7,6},{8,9},{9,8},{10,11... | collective-permute-start | bytes 786440 | tf_op jit(solution)/shard_map/ppermute | solution.py:366
  36.7 21.3 %all-to-all-start.1 = ((f32[32,24,128]{2,1,0:T(8,128)}), f32[32,24,128]{2,1,0:T(8,128)S(1)}, u32[]{:S(2)}, u32[]{:S(2)}) async-start(f32[32,24,128]{2,1,0:T(8,128)} %get-tuple-element.23), calls=%async_computation.1 | async-start | bytes 786432 | tf_op jit(solution)/shard_map/all_to_all | solution.py:29
  61.6 23.5 %copy-start = (f32[256]{0:T(256)S(1)}, f32[256]{0:T(256)}, u32[]{:S(2)}) copy-start(f32[256]{0:T(256)} %param.27) | copy-start | bytes 3076
  61.6 23.5 %all-to-all-start.2 = ((bf16[32,24,384]{2,1,0:T(8,128)(2,1)}), bf16[32,24,384]{2,1,0:T(8,128)(2,1)S(1)}, u32[]{:S(2)}, u32[]{:S(2)}) async-start(bf16[32,24,384]{2,1,0:T(8,128)(2,1)} %prompt_projection_out.1), calls=%async_computation.2 | async-start | bytes 1179648 | tf_op jit(solution)/shard_map/all_to_all | solution.py:29
  69.4 4.0 %collective-permute-start.6 = (f32[32,128]{1,0:T(8,128)S(1)}, f32[32,128]{1,0:T(8,128)S(1)}, u32[]{:S(2)}, u32[]{:S(2)}) collective-permute-start(f32[32,128]{1,0:T(8,128)S(1)} %get-tuple-element.15.lse), channel_id=1, source_target_pairs={{0,6},{2,4},{4,2},{6,0},{1,7},{3,5},{5,3},{7,1},{8,14},{10,12},{12... | collective-permute-start | bytes 49160 | tf_op jit(solution)/shard_map/ppermute | solution.py:450
  70.5 2.9 %collective-permute-start.5 = (f32[32,128]{1,0:T(8,128)S(1)}, f32[32,128]{1,0:T(8,128)S(1)}, u32[]{:S(2)}, u32[]{:S(2)}) collective-permute-start(f32[32,128]{1,0:T(8,128)S(1)} %get-tuple-element.15.lse), channel_id=1, source_target_pairs={{0,4},{2,6},{4,0},{6,2},{1,5},{3,7},{5,1},{7,3},{8,12},{10,14},{12... | collective-permute-start | bytes 49160 | tf_op jit(solution)/shard_map/ppermute | solution.py:450
  70.5 4.2 %collective-permute-start.4 = (f32[32,128]{1,0:T(8,128)S(1)}, f32[32,128]{1,0:T(8,128)S(1)}, u32[]{:S(2)}, u32[]{:S(2)}) collective-permute-start(f32[32,128]{1,0:T(8,128)S(1)} %get-tuple-element.15.lse), channel_id=1, source_target_pairs={{0,2},{2,0},{4,6},{6,4},{1,3},{3,1},{5,7},{7,5},{8,10},{10,8},{12,... | collective-permute-start | bytes 49160 | tf_op jit(solution)/shard_map/ppermute | solution.py:450
  74.7 4.5 %collective-permute-start.7 = (f32[32,128]{1,0:T(8,128)S(1)}, f32[32,128]{1,0:T(8,128)S(1)}, u32[]{:S(2)}, u32[]{:S(2)}) collective-permute-start(f32[32,128]{1,0:T(8,128)S(1)} %multiply_add_fusion.1), channel_id=1, source_target_pairs={{0,1},{1,0},{2,3},{3,2},{4,5},{5,4},{6,7},{7,6},{8,9},{9,8},{10,11... | collective-permute-start | bytes 49160 | tf_op jit(solution)/shard_map/ppermute | solution.py:452
  81.9 23.1 %copy-start.1 = (bf16[128,256]{1,0:T(8,128)(2,1)S(1)}, bf16[128,256]{1,0:T(8,128)(2,1)}, u32[]{:S(2)}) copy-start(bf16[128,256]{1,0:T(8,128)(2,1)} %refs_0_.1) | copy-start | bytes 196612
  81.9 23.1 %copy-start.3 = (f32[256]{0:T(256)S(1)}, f32[256]{0:T(256)}, u32[]{:S(2)}) copy-start(f32[256]{0:T(256)} %param.26) | copy-start | bytes 3076
  81.9 23.8 %copy-start.2 = (bf16[24,256]{1,0:T(8,128)(2,1)S(1)}, bf16[24,256]{1,0:T(8,128)(2,1)}, u32[]{:S(2)}) copy-start(bf16[24,256]{1,0:T(8,128)(2,1)} %tokens.1) | copy-start | bytes 36868
  81.9 11.2 %collective-permute-start.8 = (bf16[512,256]{1,0:T(8,128)(2,1)S(1)}, bf16[512,256]{1,0:T(8,128)(2,1)S(1)}, u32[]{:S(2)}, u32[]{:S(2)}) collective-permute-start(bf16[512,256]{1,0:T(8,128)(2,1)S(1)} %get-tuple-element.18), channel_id=1, source_target_pairs={{0,1},{1,0},{2,3},{3,2},{4,5},{5,4},{6,7},{7,6},{8,9},{9,8},{10,11... | collective-permute-start | bytes 786440 | tf_op jit(solution)/shard_map/ppermute | solution.py:521
  86.0 13.0 %all-to-all-start.3 = ((f32[8,24,256]{2,1,0:T(8,128)}), f32[8,24,256]{2,1,0:T(8,128)S(1)}, u32[]{:S(2)}, u32[]{:S(2)}) async-start(f32[8,24,256]{2,1,0:T(8,128)} %category_partial.1), calls=%async_computation.3 | async-start | bytes 393216 | tf_op jit(solution)/shard_map/all_to_all | solution.py:29
  93.2 11.7 %collective-permute-start.11 = (bf16[128,256]{1,0:T(8,128)(2,1)S(1)}, bf16[128,256]{1,0:T(8,128)(2,1)S(1)}, u32[]{:S(2)}, u32[]{:S(2)}) collective-permute-start(bf16[128,256]{1,0:T(8,128)(2,1)S(1)} %get-tuple-element.22), channel_id=1, source_target_pairs={{0,6},{2,4},{4,2},{6,0},{1,7},{3,5},{5,3},{7,1},{8,14},{10,12},{12... | collective-permute-start | bytes 196616 | tf_op jit(solution)/shard_map/ppermute | solution.py:533
  95.9 9.1 %collective-permute-start.10 = (bf16[128,256]{1,0:T(8,128)(2,1)S(1)}, bf16[128,256]{1,0:T(8,128)(2,1)S(1)}, u32[]{:S(2)}, u32[]{:S(2)}) collective-permute-start(bf16[128,256]{1,0:T(8,128)(2,1)S(1)} %get-tuple-element.21), channel_id=1, source_target_pairs={{0,4},{2,6},{4,0},{6,2},{1,5},{3,7},{5,1},{7,3},{8,12},{10,14},{12... | collective-permute-start | bytes 196616 | tf_op jit(solution)/shard_map/ppermute | solution.py:533
  95.9 9.1 %collective-permute-start.9 = (bf16[128,256]{1,0:T(8,128)(2,1)S(1)}, bf16[128,256]{1,0:T(8,128)(2,1)S(1)}, u32[]{:S(2)}, u32[]{:S(2)}) collective-permute-start(bf16[128,256]{1,0:T(8,128)(2,1)S(1)} %get-tuple-element.20), channel_id=1, source_target_pairs={{0,2},{2,0},{4,6},{6,4},{1,3},{3,1},{5,7},{7,5},{8,10},{10,8},{12,... | collective-permute-start | bytes 196616 | tf_op jit(solution)/shard_map/ppermute | solution.py:533
  99.7 14.6 %all-to-all-start.4 = ((bf16[32,24,128]{2,1,0:T(8,128)(2,1)}), bf16[32,24,128]{2,1,0:T(8,128)(2,1)S(1)}, u32[]{:S(2)}, u32[]{:S(2)}) async-start(bf16[32,24,128]{2,1,0:T(8,128)(2,1)} %category_mean.1), calls=%async_computation.4 | async-start | bytes 393216 | tf_op jit(solution)/shard_map/all_to_all | solution.py:29

commit v4 on v3

--- a/solution.py
+++ b/solution.py
@@ -241,22 +241,25 @@
                 ]
 
 
-def category_kernel(place, arrived, packed, scale, out):
-    _, rows, wide = arrived.shape
-    depth = wide - 128
+def base_kernel(place, packed, base, tally):
+    rows = base.shape[0]
     group, side = place[0] // 2, place[0] % 2
     members = members_of(codes_of(packed), group * rows, rows)
-    base = dot(members.astype(BF), tokens_of(packed))
-    own = jnp.where(side == 0, base[:, :128], base[:, 128:])
-    factor = jnp.where(side == 0, scale[:, :128], scale[:, 128:])
-    sums = own + factor * jnp.sum(arrived[:, :, depth:].astype(F32), axis=0)
-    tally = jnp.broadcast_to(jnp.sum(members, axis=1, keepdims=True), sums.shape)
-    out[:, :, :128] = jnp.broadcast_to(sums[None], (out.shape[0], rows, 128))
-    out[:, :, 128:] = jnp.broadcast_to(tally[None], (out.shape[0], rows, 128))
-
-
-def mean_kernel(partials, out):
-    sums = jnp.sum(partials[...], axis=0)
+    wide = dot(members.astype(BF), tokens_of(packed))
+    base[...] = jnp.where(side == 0, wide[:, :128], wide[:, 128:])
+    tally[...] = jnp.broadcast_to(jnp.sum(members, axis=1, keepdims=True), tally.shape)
+
+
+def category_kernel(place, arrived, base, tally, scale, out):
+    wide = arrived.shape[2]
+    factor = jnp.where(place[0] % 2 == 0, scale[:, :128], scale[:, 128:])
+    out[:, :128] = base[...] + factor * jnp.sum(arrived[:, :, wide - 128 :].astype(F32), axis=0)
+    out[:, 128:] = tally[...]
+
+
+def mean_kernel(*refs):
+    *parts, out = refs
+    sums = sum(part[...] for part in parts)
     out[...] = jnp.broadcast_to((sums[:, :128] / sums[:, 128:]).astype(BF)[None], out.shape)
 
 
@@ -490,26 +493,39 @@
         name="image_projection_out",
     )(core, row_whole, row_lse, *kept_far(image_part_t, image_out_weight))
 
-    category_copies = pl.pallas_call(
+    plane_place = lax.axis_index(PLANE).astype(jnp.int32).reshape(1)
+    base, tally = pl.pallas_call(
+        base_kernel,
+        in_specs=[scalar, pl.BlockSpec(memory_space=pltpu.VMEM)],
+        out_shape=[shaped((own_prompts, 128), F32)] * 2,
+        compiler_params=params(),
+        cost_estimate=cost(2 * own_prompts * prompts * depth, 4 * prompts * depth),
+        name="category_base",
+    )(plane_place, prompt_all)
+    category_own = pl.pallas_call(
         category_kernel,
-        in_specs=[scalar] + [pl.BlockSpec(memory_space=pltpu.VMEM)] * 3,
-        out_shape=shaped((columns, own_prompts, depth), F32),
+        in_specs=[scalar] + [pl.BlockSpec(memory_space=pltpu.VMEM)] * 4,
+        out_shape=shaped((own_prompts, depth), F32),
         compiler_params=params(),
         cost_estimate=cost(2 * own_prompts * prompts * depth, 4 * prompts * depth),
         name="category_partial",
     )(
-        lax.axis_index(PLANE).astype(jnp.int32).reshape(1),
+        plane_place,
         plane_arrived,
-        prompt_all,
+        base,
+        tally,
         prompt_layer_scale.reshape(1, depth),
     )
-    partials = swap(category_copies, COLUMN)
+    core_sum = category_own + lax.ppermute(category_own, CORE, swapped)
+    line_sums = [core_sum]
+    for k in range(1, line):
+        line_sums.append(lax.ppermute(core_sum, LINE, [(i, i ^ k) for i in range(line)]))
     mean_copies = pl.pallas_call(
         mean_kernel,
         out_shape=shaped((planes, own_prompts, 128), BF),
         compiler_params=params(),
         name="category_mean",
-    )(partials)
+    )(*line_sums)
     mean_all = swap(mean_copies, PLANE)
     category_embed = pl.pallas_call(
         table_kernel,

time: 117 us -> 121 us (1.034)
  the two profiles are of different devices: /device:TPU:1 before, /device:TPU:32 now
where the time goes in v4:
time: 121 us; the launch traced here: 120 us
  starting transfers between devices  45.1 us (37%)
  waiting for transfers between devices  42.1 us (35%)
  Pallas kernels  30.7 us (25%)
  other arithmetic  1.42 us (1%)
    all_to_all x4, starting transfers between devices, swap(): return lax.all_to_all(parts, axes, split_axis=0, concat_axis=0, tiled=True)  27 us
    all_to_all x4, waiting for transfers between devices, swap(): return lax.all_to_all(parts, axes, split_axis=0, concat_axis=0, tiled=True)  24.5 us
    pallas_call x1, Pallas kernels, on_device(): pl.pallas_call(row_kernel, grid=(heads,), in_specs=[scalar, whole(image_o...  10.3 us
    pallas_call x1, Pallas kernels, on_device(): pl.pallas_call(column_kernel, grid=(heads,), in_specs=[scalar, whole(imag...  9.62 us
    ppermute x3, waiting for transfers between devices, on_device(): lax.ppermute(core_sum, LINE, [(i, i ^ k) for i in range(line)])  6.98 us
    ppermute x3, waiting for transfers between devices, on_device(): lax.ppermute(image_tokens, LINE, [(i, i ^ k) for i in range(line)])  5.31 us
    ppermute x3, starting transfers between devices, on_device(): lax.ppermute(row_lse, LINE, [(i, i ^ k) for i in range(line)])  4.79 us
    ppermute x3, starting transfers between devices, on_device(): image_delta += lax.ppermute(image_sent[k], LINE, turned).astype(F32)  4.79 us
  transfers between devices with their start and end apart: 20, of which 14 were waited for; matrix products, arithmetic and copies ran while one was open for 1% of the time, Pallas kernels for 13%

profile of v4, /device:TPU:32, one launch (start us, length us, event | category | flops | bytes accessed | tf_op | source)
XLA Modules:
  0.0 120.1 jit_solution(6285641780857043217)
XLA Ops:
  0.6 1.6 %pack.1 = bf16[32,56,128]{2,1,0:T(8,128)(2,1)} custom-call(bf16[24,256]{1,0:T(8,128)(2,1)} %tokens.1, s32[1,24]{1,0:T(1,128)} %bitcast.10, s32[1,24]{1,0:T(1,128)} %bitcast.11), custom_call_target="tpu_custom_call" | custom-call | tf_op jit(solution)/shard_map/pack/pallas_call | solution.py:334
  2.2 11.2 %all-to-all-start = ((bf16[32,56,128]{2,1,0:T(8,128)(2,1)}), bf16[32,56,128]{2,1,0:T(8,128)(2,1)S(1)}, u32[]{:S(2)}, u32[]{:S(2)}) async-start(bf16[32,56,128]{2,1,0:T(8,128)(2,1)} %pack.1), calls=%async_computation | async-start | bytes 917504 | tf_op jit(solution)/shard_map/all_to_all | solution.py:29
  13.4 3.3 %collective-permute-start = (bf16[128,256]{1,0:T(8,128)(2,1)}, bf16[128,256]{1,0:T(8,128)(2,1)S(1)}, u32[]{:S(2)}, u32[]{:S(2)}) collective-permute-start(bf16[128,256]{1,0:T(8,128)(2,1)} %refs_0_.1), channel_id=1, source_target_pairs={{0,2},{2,0},{4,6},{6,4},{1,3},{3,1},{5,7},{7,5},{8,10},{10,8},{12,... | collective-permute-start | bytes 196616 | tf_op jit(solution)/shard_map/ppermute | solution.py:346
  16.7 0.7 collective-permute-start.1
  17.4 0.4 collective-permute-start.2
  17.8 2.2 %collective-permute-done.refs_1_ = bf16[128,256]{1,0:T(8,128)(2,1)S(1)} collective-permute-done((bf16[128,256]{1,0:T(8,128)(2,1)}, bf16[128,256]{1,0:T(8,128)(2,1)S(1)}, u32[]{:S(2)}, u32[]{:S(2)}) %collective-permute-start) | collective-permute-done | bytes 65568 | tf_op jit(solution)/shard_map/ppermute | solution.py:346
  20.0 1.2 collective-permute-done.1.refs_2_
  21.2 1.9 %collective-permute-done.2.refs_3_ = bf16[128,256]{1,0:T(8,128)(2,1)S(1)} collective-permute-done((bf16[128,256]{1,0:T(8,128)(2,1)}, bf16[128,256]{1,0:T(8,128)(2,1)S(1)}, u32[]{:S(2)}, u32[]{:S(2)}) %collective-permute-start.2) | collective-permute-done | bytes 65568 | tf_op jit(solution)/shard_map/ppermute | solution.py:346
  23.1 1.1 image_norm.1.own
  24.1 0.1 collective-permute-start.3
  24.2 1.5 %collective-permute-done.3.other = bf16[512,256]{1,0:T(8,128)(2,1)S(1)} collective-permute-done((bf16[512,256]{1,0:T(8,128)(2,1)S(1)}, bf16[512,256]{1,0:T(8,128)(2,1)S(1)}, u32[]{:S(2)}, u32[]{:S(2)}) %collective-permute-start.3) | collective-permute-done | bytes 262176 | tf_op jit(solution)/shard_map/ppermute | solution.py:369
  25.8 3.9 %all-to-all-done.packed = bf16[32,56,128]{2,1,0:T(8,128)(2,1)S(1)} async-done(((bf16[32,56,128]{2,1,0:T(8,128)(2,1)}), bf16[32,56,128]{2,1,0:T(8,128)(2,1)S(1)}, u32[]{:S(2)}, u32[]{:S(2)}) %all-to-all-start) | async-done | bytes 458784 | tf_op jit(solution)/shard_map/all_to_all | solution.py:29
  29.6 9.6 %column_attention.1 = (bf16[1024,768]{1,0:T(8,128)(2,1)}, f32[24,128]{1,0:T(8,128)S(1)}, f32[32,24,128]{2,1,0:T(8,128)}) custom-call(s32[1]{0:T(128)} %bitcast.1.core, bf16[512,256]{1,0:T(8,128)(2,1)S(1)} %image_norm.1.own, bf16[512,256]{1,0:T(8,128)(2,1)S(1)} %collective-permute-done.3.other, bf16[32,56,128]{2,1,0:T(8,128)(2,1)S(1)} %all-to-all-done.packed, ...), custom_call_target="tpu_custom_call" | custom-call | flops 6442450944 | bytes 6291456 | tf_op jit(solution)/shard_map/column_attention/pallas_call | solution.py:370
  39.3 5.9 %all-to-all-start.1 = ((f32[32,24,128]{2,1,0:T(8,128)}), f32[32,24,128]{2,1,0:T(8,128)S(1)}, u32[]{:S(2)}, u32[]{:S(2)}) async-start(f32[32,24,128]{2,1,0:T(8,128)} %get-tuple-element.25), calls=%async_computation.1 | async-start | bytes 786432 | tf_op jit(solution)/shard_map/all_to_all | solution.py:29
  45.2 10.3 %row_attention.1 = (bf16[1024,1024]{1,0:T(8,128)(2,1)}, f32[32,128]{1,0:T(8,128)S(1)}, bf16[384,768]{1,0:T(8,128)(2,1)}) custom-call(s32[1]{0:T(128)} %bitcast.1.core, bf16[512,256]{1,0:T(8,128)(2,1)S(1)} %image_norm.1.own, bf16[512,256]{1,0:T(8,128)(2,1)S(1)} %collective-permute-done.3.other, bf16[32,56,128]{2,1,0:T(8,128)(2,1)S(1)} %all-to-all-done.packed, ...), custom_call_target="tpu_custom_call" | custom-call | flops 6442450944 | bytes 6291456 | tf_op jit(solution)/shard_map/row_attention/pallas_call | solution.py:408
  55.5 5.0 %all-to-all-done.1.lse_all = f32[32,24,128]{2,1,0:T(8,128)S(1)} async-done(((f32[32,24,128]{2,1,0:T(8,128)}), f32[32,24,128]{2,1,0:T(8,128)S(1)}, u32[]{:S(2)}, u32[]{:S(2)}) %all-to-all-start.1) | async-done | bytes 393248 | tf_op jit(solution)/shard_map/all_to_all | solution.py:29
  60.5 3.6 %prompt_projection_out.1 = bf16[32,24,384]{2,1,0:T(8,128)(2,1)} custom-call(f32[32,24,128]{2,1,0:T(8,128)S(1)} %all-to-all-done.1.lse_all, f32[24,128]{1,0:T(8,128)S(1)} %get-tuple-element.26.lse, bf16[1024,768]{1,0:T(8,128)(2,1)} %get-tuple-element.27.out_t, bf16[1024,256]{1,0:T(8,128)(2,1)} %out_w.3, bf16[384,768]{1,0:T(8,128)(2,1)} %get-tuple-element.28.members), custom_call_target="tpu_custom_call" | custom-call | flops 553648128 | bytes 4718592 | tf_op jit(solution)/shard_map/prompt_projection_out/pallas_call | solution.py:457
  64.0 0.0 copy-start
  64.1 4.9 %all-to-all-start.2 = ((bf16[32,24,384]{2,1,0:T(8,128)(2,1)}), bf16[32,24,384]{2,1,0:T(8,128)(2,1)S(1)}, u32[]{:S(2)}, u32[]{:S(2)}) async-start(bf16[32,24,384]{2,1,0:T(8,128)(2,1)} %prompt_projection_out.1), calls=%async_computation.2 | async-start | bytes 1179648 | tf_op jit(solution)/shard_map/all_to_all | solution.py:29
  69.0 2.0 %collective-permute-start.6 = (f32[32,128]{1,0:T(8,128)S(1)}, f32[32,128]{1,0:T(8,128)S(1)}, u32[]{:S(2)}, u32[]{:S(2)}) collective-permute-start(f32[32,128]{1,0:T(8,128)S(1)} %get-tuple-element.17.lse), channel_id=1, source_target_pairs={{0,6},{2,4},{4,2},{6,0},{1,7},{3,5},{5,3},{7,1},{8,14},{10,12},{12... | collective-permute-start | bytes 49160 | tf_op jit(solution)/shard_map/ppermute | solution.py:453
  71.0 0.1 collective-permute-start.5
  71.1 2.6 %collective-permute-start.4 = (f32[32,128]{1,0:T(8,128)S(1)}, f32[32,128]{1,0:T(8,128)S(1)}, u32[]{:S(2)}, u32[]{:S(2)}) collective-permute-start(f32[32,128]{1,0:T(8,128)S(1)} %get-tuple-element.17.lse), channel_id=1, source_target_pairs={{0,2},{2,0},{4,6},{6,4},{1,3},{3,1},{5,7},{7,5},{8,10},{10,8},{12,... | collective-permute-start | bytes 49160 | tf_op jit(solution)/shard_map/ppermute | solution.py:453
  73.8 0.2 collective-permute-done.6
  74.0 0.7 collective-permute-done.5
  74.7 1.6 %collective-permute-done.4 = f32[32,128]{1,0:T(8,128)S(1)} collective-permute-done((f32[32,128]{1,0:T(8,128)S(1)}, f32[32,128]{1,0:T(8,128)S(1)}, u32[]{:S(2)}, u32[]{:S(2)}) %collective-permute-start.4) | collective-permute-done | bytes 16416 | tf_op jit(solution)/shard_map/ppermute | solution.py:453
  76.4 0.3 collective-permute-start.7
  76.7 1.2 collective-permute-done.7
  77.9 0.0 copy-start.1
  77.9 0.0 copy-start.3
  77.9 2.7 %image_projection_out.1 = (bf16[512,256]{1,0:T(8,128)(2,1)S(1)}, bf16[512,256]{1,0:T(8,128)(2,1)S(1)}) custom-call(s32[1]{0:T(128)} %bitcast.1.core, f32[32,128]{1,0:T(8,128)S(1)} %multiply_add_fusion.lse_whole, f32[32,128]{1,0:T(8,128)S(1)} %get-tuple-element.17.lse, bf16[1024,1024]{1,0:T(8,128)(2,1)} %get-tuple-element.18.out_t, bf16[1024,256]{1,0:T(8,128)(2,1)} %out_w.2), custom_call_target="tpu_custom_call" | custom-call | flops 536870912 | bytes 6291456 | tf_op jit(solution)/shard_map/image_projection_out/pallas_call | solution.py:480
  80.6 0.0 copy-start.2
  80.6 0.3 collective-permute-start.8
  80.9 0.3 category_base.1
  81.2 6.5 %all-to-all-done.2.arrived = bf16[32,24,384]{2,1,0:T(8,128)(2,1)S(1)} async-done(((bf16[32,24,384]{2,1,0:T(8,128)(2,1)}), bf16[32,24,384]{2,1,0:T(8,128)(2,1)S(1)}, u32[]{:S(2)}, u32[]{:S(2)}) %all-to-all-start.2) | async-done | bytes 589856 | tf_op jit(solution)/shard_map/all_to_all | solution.py:29
  87.7 0.0 copy-done
  87.7 0.1 collective-permute-start.12
  87.8 0.0 collective-permute-done.8.arrived
  87.8 0.1 image_sum.1
  87.9 1.4 %collective-permute-start.11 = (bf16[128,256]{1,0:T(8,128)(2,1)S(1)}, bf16[128,256]{1,0:T(8,128)(2,1)S(1)}, u32[]{:S(2)}, u32[]{:S(2)}) collective-permute-start(bf16[128,256]{1,0:T(8,128)(2,1)S(1)} %get-tuple-element.24), channel_id=1, source_target_pairs={{0,6},{2,4},{4,2},{6,0},{1,7},{3,5},{5,3},{7,1},{8,14},{10,12},{12... | collective-permute-start | bytes 196616 | tf_op jit(solution)/shard_map/ppermute | solution.py:549
  89.3 0.1 collective-permute-start.10
  89.4 3.3 %collective-permute-start.9 = (bf16[128,256]{1,0:T(8,128)(2,1)S(1)}, bf16[128,256]{1,0:T(8,128)(2,1)S(1)}, u32[]{:S(2)}, u32[]{:S(2)}) collective-permute-start(bf16[128,256]{1,0:T(8,128)(2,1)S(1)} %get-tuple-element.22), channel_id=1, source_target_pairs={{0,2},{2,0},{4,6},{6,4},{1,3},{3,1},{5,7},{7,5},{8,10},{10,8},{12,... | collective-permute-start | bytes 196616 | tf_op jit(solution)/shard_map/ppermute | solution.py:549
  92.7 0.0 collective-permute-done.12
  92.7 0.3 collective-permute-start.13
  93.0 1.9 %collective-permute-start.14 = (f32[24,256]{1,0:T(8,128)S(1)}, f32[24,256]{1,0:T(8,128)S(1)}, u32[]{:S(2)}, u32[]{:S(2)}) collective-permute-start(f32[24,256]{1,0:T(8,128)S(1)} %add.55.refs_0_), channel_id=1, source_target_pairs={{0,4},{2,6},{4,0},{6,2},{1,5},{3,7},{5,1},{7,3},{8,12},{10,14},{12... | collective-permute-start | bytes 73736 | tf_op jit(solution)/shard_map/ppermute | solution.py:522
  94.9 3.2 %collective-permute-done.13.refs_1_ = f32[24,256]{1,0:T(8,128)S(1)} collective-permute-done((f32[24,256]{1,0:T(8,128)S(1)}, f32[24,256]{1,0:T(8,128)S(1)}, u32[]{:S(2)}, u32[]{:S(2)}) %collective-permute-start.13) | collective-permute-done | bytes 24608 | tf_op jit(solution)/shard_map/ppermute | solution.py:522
  98.1 1.3 %collective-permute-start.15 = (f32[24,256]{1,0:T(8,128)S(1)}, f32[24,256]{1,0:T(8,128)S(1)}, u32[]{:S(2)}, u32[]{:S(2)}) collective-permute-start(f32[24,256]{1,0:T(8,128)S(1)} %add.55.refs_0_), channel_id=1, source_target_pairs={{0,6},{2,4},{4,2},{6,0},{1,7},{3,5},{5,3},{7,1},{8,14},{10,12},{12... | collective-permute-start | bytes 73736 | tf_op jit(solution)/shard_map/ppermute | solution.py:522
  99.4 0.0 collective-permute-done.14.refs_2_
  99.4 3.8 %collective-permute-done.15.refs_3_ = f32[24,256]{1,0:T(8,128)S(1)} collective-permute-done((f32[24,256]{1,0:T(8,128)S(1)}, f32[24,256]{1,0:T(8,128)S(1)}, u32[]{:S(2)}, u32[]{:S(2)}) %collective-permute-start.15) | collective-permute-done | bytes 24608 | tf_op jit(solution)/shard_map/ppermute | solution.py:522
  103.2 0.7 category_mean.1
  103.9 4.9 %all-to-all-start.3 = ((bf16[32,24,128]{2,1,0:T(8,128)(2,1)}), bf16[32,24,128]{2,1,0:T(8,128)(2,1)S(1)}, u32[]{:S(2)}, u32[]{:S(2)}) async-start(bf16[32,24,128]{2,1,0:T(8,128)(2,1)} %category_mean.1), calls=%async_computation.3 | async-start | bytes 393216 | tf_op jit(solution)/shard_map/all_to_all | solution.py:29
  108.8 0.0 collective-permute-done.11
  108.8 0.0 collective-permute-done.10
  108.8 0.0 collective-permute-done.9
  108.8 0.0 copy-done.1
  108.8 0.0 copy-done.3
  108.9 0.7 add_convert_fusion
  109.5 0.1 convert_reduce_fusion
  109.6 0.0 copy-done.2
  109.6 0.6 add_convert_fusion.1
  110.2 9.1 %all-to-all-done.3.pieces = bf16[32,24,128]{2,1,0:T(8,128)(2,1)S(1)} async-done(((bf16[32,24,128]{2,1,0:T(8,128)(2,1)}), bf16[32,24,128]{2,1,0:T(8,128)(2,1)S(1)}, u32[]{:S(2)}, u32[]{:S(2)}) %all-to-all-start.3) | async-done | bytes 196640 | tf_op jit(solution)/shard_map/all_to_all | solution.py:29
  119.3 0.8 category_table.1
  (4 shorter events, 0.1 us)
Async XLA Ops:
  2.2 27.4 %all-to-all-start = ((bf16[32,56,128]{2,1,0:T(8,128)(2,1)}), bf16[32,56,128]{2,1,0:T(8,128)(2,1)S(1)}, u32[]{:S(2)}, u32[]{:S(2)}) async-start(bf16[32,56,128]{2,1,0:T(8,128)(2,1)} %pack.1), calls=%async_computation | async-start | bytes 917504 | tf_op jit(solution)/shard_map/all_to_all | solution.py:29
  13.4 6.6 %collective-permute-start = (bf16[128,256]{1,0:T(8,128)(2,1)}, bf16[128,256]{1,0:T(8,128)(2,1)S(1)}, u32[]{:S(2)}, u32[]{:S(2)}) collective-permute-start(bf16[128,256]{1,0:T(8,128)(2,1)} %refs_0_.1), channel_id=1, source_target_pairs={{0,2},{2,0},{4,6},{6,4},{1,3},{3,1},{5,7},{7,5},{8,10},{10,8},{12,... | collective-permute-start | bytes 196616 | tf_op jit(solution)/shard_map/ppermute | solution.py:346
  16.7 4.5 %collective-permute-start.1 = (bf16[128,256]{1,0:T(8,128)(2,1)}, bf16[128,256]{1,0:T(8,128)(2,1)S(1)}, u32[]{:S(2)}, u32[]{:S(2)}) collective-permute-start(bf16[128,256]{1,0:T(8,128)(2,1)} %refs_0_.1), channel_id=1, source_target_pairs={{0,4},{2,6},{4,0},{6,2},{1,5},{3,7},{5,1},{7,3},{8,12},{10,14},{12... | collective-permute-start | bytes 196616 | tf_op jit(solution)/shard_map/ppermute | solution.py:346
  17.4 5.7 %collective-permute-start.2 = (bf16[128,256]{1,0:T(8,128)(2,1)}, bf16[128,256]{1,0:T(8,128)(2,1)S(1)}, u32[]{:S(2)}, u32[]{:S(2)}) collective-permute-start(bf16[128,256]{1,0:T(8,128)(2,1)} %refs_0_.1), channel_id=1, source_target_pairs={{0,6},{2,4},{4,2},{6,0},{1,7},{3,5},{5,3},{7,1},{8,14},{10,12},{12... | collective-permute-start | bytes 196616 | tf_op jit(solution)/shard_map/ppermute | solution.py:346
  24.1 1.6 %collective-permute-start.3 = (bf16[512,256]{1,0:T(8,128)(2,1)S(1)}, bf16[512,256]{1,0:T(8,128)(2,1)S(1)}, u32[]{:S(2)}, u32[]{:S(2)}) collective-permute-start(bf16[512,256]{1,0:T(8,128)(2,1)S(1)} %image_norm.1.own), channel_id=1, source_target_pairs={{0,1},{1,0},{2,3},{3,2},{4,5},{5,4},{6,7},{7,6},{8,9},{9,8},{10,11... | collective-permute-start | bytes 786440 | tf_op jit(solution)/shard_map/ppermute | solution.py:369
  39.3 21.2 %all-to-all-start.1 = ((f32[32,24,128]{2,1,0:T(8,128)}), f32[32,24,128]{2,1,0:T(8,128)S(1)}, u32[]{:S(2)}, u32[]{:S(2)}) async-start(f32[32,24,128]{2,1,0:T(8,128)} %get-tuple-element.25), calls=%async_computation.1 | async-start | bytes 786432 | tf_op jit(solution)/shard_map/all_to_all | solution.py:29
  64.0 23.6 %copy-start = (f32[256]{0:T(256)S(1)}, f32[256]{0:T(256)}, u32[]{:S(2)}) copy-start(f32[256]{0:T(256)} %param.27) | copy-start | bytes 3076
  64.1 23.6 %all-to-all-start.2 = ((bf16[32,24,384]{2,1,0:T(8,128)(2,1)}), bf16[32,24,384]{2,1,0:T(8,128)(2,1)S(1)}, u32[]{:S(2)}, u32[]{:S(2)}) async-start(bf16[32,24,384]{2,1,0:T(8,128)(2,1)} %prompt_projection_out.1), calls=%async_computation.2 | async-start | bytes 1179648 | tf_op jit(solution)/shard_map/all_to_all | solution.py:29
  69.0 5.0 %collective-permute-start.6 = (f32[32,128]{1,0:T(8,128)S(1)}, f32[32,128]{1,0:T(8,128)S(1)}, u32[]{:S(2)}, u32[]{:S(2)}) collective-permute-start(f32[32,128]{1,0:T(8,128)S(1)} %get-tuple-element.17.lse), channel_id=1, source_target_pairs={{0,6},{2,4},{4,2},{6,0},{1,7},{3,5},{5,3},{7,1},{8,14},{10,12},{12... | collective-permute-start | bytes 49160 | tf_op jit(solution)/shard_map/ppermute | solution.py:453
  71.0 3.7 %collective-permute-start.5 = (f32[32,128]{1,0:T(8,128)S(1)}, f32[32,128]{1,0:T(8,128)S(1)}, u32[]{:S(2)}, u32[]{:S(2)}) collective-permute-start(f32[32,128]{1,0:T(8,128)S(1)} %get-tuple-element.17.lse), channel_id=1, source_target_pairs={{0,4},{2,6},{4,0},{6,2},{1,5},{3,7},{5,1},{7,3},{8,12},{10,14},{12... | collective-permute-start | bytes 49160 | tf_op jit(solution)/shard_map/ppermute | solution.py:453
  71.1 5.2 %collective-permute-start.4 = (f32[32,128]{1,0:T(8,128)S(1)}, f32[32,128]{1,0:T(8,128)S(1)}, u32[]{:S(2)}, u32[]{:S(2)}) collective-permute-start(f32[32,128]{1,0:T(8,128)S(1)} %get-tuple-element.17.lse), channel_id=1, source_target_pairs={{0,2},{2,0},{4,6},{6,4},{1,3},{3,1},{5,7},{7,5},{8,10},{10,8},{12,... | collective-permute-start | bytes 49160 | tf_op jit(solution)/shard_map/ppermute | solution.py:453
  76.4 1.5 %collective-permute-start.7 = (f32[32,128]{1,0:T(8,128)S(1)}, f32[32,128]{1,0:T(8,128)S(1)}, u32[]{:S(2)}, u32[]{:S(2)}) collective-permute-start(f32[32,128]{1,0:T(8,128)S(1)} %multiply_add_fusion.1), channel_id=1, source_target_pairs={{0,1},{1,0},{2,3},{3,2},{4,5},{5,4},{6,7},{7,6},{8,9},{9,8},{10,11... | collective-permute-start | bytes 49160 | tf_op jit(solution)/shard_map/ppermute | solution.py:455
  77.9 30.9 %copy-start.1 = (bf16[128,256]{1,0:T(8,128)(2,1)S(1)}, bf16[128,256]{1,0:T(8,128)(2,1)}, u32[]{:S(2)}) copy-start(bf16[128,256]{1,0:T(8,128)(2,1)} %refs_0_.1) | copy-start | bytes 196612
  77.9 30.9 %copy-start.3 = (f32[256]{0:T(256)S(1)}, f32[256]{0:T(256)}, u32[]{:S(2)}) copy-start(f32[256]{0:T(256)} %param.26) | copy-start | bytes 3076
  80.6 29.0 %copy-start.2 = (bf16[24,256]{1,0:T(8,128)(2,1)S(1)}, bf16[24,256]{1,0:T(8,128)(2,1)}, u32[]{:S(2)}) copy-start(bf16[24,256]{1,0:T(8,128)(2,1)} %tokens.1) | copy-start | bytes 36868
  80.6 7.2 %collective-permute-start.8 = (bf16[512,256]{1,0:T(8,128)(2,1)S(1)}, bf16[512,256]{1,0:T(8,128)(2,1)S(1)}, u32[]{:S(2)}, u32[]{:S(2)}) collective-permute-start(bf16[512,256]{1,0:T(8,128)(2,1)S(1)} %get-tuple-element.20), channel_id=1, source_target_pairs={{0,1},{1,0},{2,3},{3,2},{4,5},{5,4},{6,7},{7,6},{8,9},{9,8},{10,11... | collective-permute-start | bytes 786440 | tf_op jit(solution)/shard_map/ppermute | solution.py:537
  87.7 5.0 %collective-permute-start.12 = (f32[24,256]{1,0:T(8,128)S(1)}, f32[24,256]{1,0:T(8,128)S(1)}, u32[]{:S(2)}, u32[]{:S(2)}) collective-permute-start(f32[24,256]{1,0:T(8,128)S(1)} %category_partial.1), channel_id=1, source_target_pairs={{0,1},{1,0},{2,3},{3,2},{4,5},{5,4},{6,7},{7,6},{8,9},{9,8},{10,11... | collective-permute-start | bytes 73736 | tf_op jit(solution)/shard_map/ppermute | solution.py:519
  87.9 20.9 %collective-permute-start.11 = (bf16[128,256]{1,0:T(8,128)(2,1)S(1)}, bf16[128,256]{1,0:T(8,128)(2,1)S(1)}, u32[]{:S(2)}, u32[]{:S(2)}) collective-permute-start(bf16[128,256]{1,0:T(8,128)(2,1)S(1)} %get-tuple-element.24), channel_id=1, source_target_pairs={{0,6},{2,4},{4,2},{6,0},{1,7},{3,5},{5,3},{7,1},{8,14},{10,12},{12... | collective-permute-start | bytes 196616 | tf_op jit(solution)/shard_map/ppermute | solution.py:549
  89.3 19.6 %collective-permute-start.10 = (bf16[128,256]{1,0:T(8,128)(2,1)S(1)}, bf16[128,256]{1,0:T(8,128)(2,1)S(1)}, u32[]{:S(2)}, u32[]{:S(2)}) collective-permute-start(bf16[128,256]{1,0:T(8,128)(2,1)S(1)} %get-tuple-element.23), channel_id=1, source_target_pairs={{0,4},{2,6},{4,0},{6,2},{1,5},{3,7},{5,1},{7,3},{8,12},{10,14},{12... | collective-permute-start | bytes 196616 | tf_op jit(solution)/shard_map/ppermute | solution.py:549
  89.4 19.4 %collective-permute-start.9 = (bf16[128,256]{1,0:T(8,128)(2,1)S(1)}, bf16[128,256]{1,0:T(8,128)(2,1)S(1)}, u32[]{:S(2)}, u32[]{:S(2)}) collective-permute-start(bf16[128,256]{1,0:T(8,128)(2,1)S(1)} %get-tuple-element.22), channel_id=1, source_target_pairs={{0,2},{2,0},{4,6},{6,4},{1,3},{3,1},{5,7},{7,5},{8,10},{10,8},{12,... | collective-permute-start | bytes 196616 | tf_op jit(solution)/shard_map/ppermute | solution.py:549
  92.7 5.4 %collective-permute-start.13 = (f32[24,256]{1,0:T(8,128)S(1)}, f32[24,256]{1,0:T(8,128)S(1)}, u32[]{:S(2)}, u32[]{:S(2)}) collective-permute-start(f32[24,256]{1,0:T(8,128)S(1)} %add.55.refs_0_), channel_id=1, source_target_pairs={{0,2},{2,0},{4,6},{6,4},{1,3},{3,1},{5,7},{7,5},{8,10},{10,8},{12,... | collective-permute-start | bytes 73736 | tf_op jit(solution)/shard_map/ppermute | solution.py:522
  93.0 6.4 %collective-permute-start.14 = (f32[24,256]{1,0:T(8,128)S(1)}, f32[24,256]{1,0:T(8,128)S(1)}, u32[]{:S(2)}, u32[]{:S(2)}) collective-permute-start(f32[24,256]{1,0:T(8,128)S(1)} %add.55.refs_0_), channel_id=1, source_target_pairs={{0,4},{2,6},{4,0},{6,2},{1,5},{3,7},{5,1},{7,3},{8,12},{10,14},{12... | collective-permute-start | bytes 73736 | tf_op jit(solution)/shard_map/ppermute | solution.py:522
  98.1 5.0 %collective-permute-start.15 = (f32[24,256]{1,0:T(8,128)S(1)}, f32[24,256]{1,0:T(8,128)S(1)}, u32[]{:S(2)}, u32[]{:S(2)}) collective-permute-start(f32[24,256]{1,0:T(8,128)S(1)} %add.55.refs_0_), channel_id=1, source_target_pairs={{0,6},{2,4},{4,2},{6,0},{1,7},{3,5},{5,3},{7,1},{8,14},{10,12},{12... | collective-permute-start | bytes 73736 | tf_op jit(solution)/shard_map/ppermute | solution.py:522
  103.9 15.4 %all-to-all-start.3 = ((bf16[32,24,128]{2,1,0:T(8,128)(2,1)}), bf16[32,24,128]{2,1,0:T(8,128)(2,1)S(1)}, u32[]{:S(2)}, u32[]{:S(2)}) async-start(bf16[32,24,128]{2,1,0:T(8,128)(2,1)} %category_mean.1), calls=%async_computation.3 | async-start | bytes 393216 | tf_op jit(solution)/shard_map/all_to_all | solution.py:29
